TPU v7x, 128 devices: a whole 4x4x4 slice. The times are simulated.
128 devices in a mesh: comp: 128 (over z, y, x, core).
Axes of the slice: x: 4, y: 4, z: 4, core: 2. Of those that a mesh axis runs over, the one named last changes fastest.
Arguments:
- src_fields: float32 [32768, 320], P('comp'), may hold values from -6 to 6
- weights: float32 [512, 256, 512], P('comp'), may hold values from -0.25 to 0.25
- block_src: int32 [512, 512], P('comp'), may hold values from 0 to 1023, as said below
- send_src: int32 [16384, 8], P('comp'), may hold values from 0 to 255, as said below
- coupler_send: int32 [16384, 16], P('comp'), may hold values from 0 to 1023, as said below
- ocean_from: int32 [131072], P('comp'), may hold values from 0 to 2047, as said below
- surface_temp: float32 [131072], P('comp'), may hold values from -4 to 4
- ocean_current: float32 [2, 131072], P(None, 'comp'), may hold values from -3 to 3
Outputs:
- remapped: float32 [131072, 320], P('comp')
- fluxes: float32 [4, 131072], P(None, 'comp')
Inputs may be any that keep to these rules, and one draw needn't show every extreme that they name: `block_src`: slots at positions below the pair's row count hold data; counts from one source device to one coupler reach 8 for some pair in every row and column of the count table, every coupler receives 2 * 256 rows, every block column names a filled slot, and every coupler's and every source device's counts form the same multiset. `send_src`: entries within one row are distinct. `coupler_send`: each coupler sends each of its 1024 rows exactly once; counts from one coupler to one ocean device reach 16 in every row and column of the count table and form the same multiset for every coupler and every ocean device; unfilled slots hold 0. `ocean_from`: each ocean device's entries are its 1024 filled receive slots, each once.
All inputs are finite; a program needn't handle non-finite values.
Results may differ from a plain program's by a relative error of at most 0.0003.
Values sent between devices are 32-bit elements; how exact they have to be, the bound alone decides.
No kernel may reach another device: no remote copies, remote signals or barrier semaphores. Data moves between devices by JAX's collectives and lax.ppermute only.
A program may use at most 64 MiB of HBM per device.

v0:
```python
import jax
import jax.numpy as jnp
from jax import lax
from jax.sharding import PartitionSpec as P

LEV = 8


def shards(
    src_fields, weights, block_src, send_src, coupler_send, ocean_from, surface_temp, ocean_current
):
    devices = lax.axis_size("comp")
    capacity = send_src.shape[1]
    blocks, block_rows, block_cols = weights.shape
    outgoing = jnp.take(src_fields, send_src, axis=0)
    received = lax.all_to_all(outgoing, "comp", split_axis=0, concat_axis=0, tiled=True)
    columns = received.shape[2]
    flat_rows = received.reshape(devices * capacity, columns)
    picked = jnp.take(flat_rows, block_src, axis=0)
    coupled = jnp.einsum(
        "bos,bsw->bow",
        weights,
        picked,
        precision=lax.Precision.HIGHEST,
        preferred_element_type=jnp.float32,
    )
    coupled = coupled.reshape(blocks * block_rows, columns)
    leaving = jnp.take(coupled, coupler_send, axis=0)
    arrived = lax.all_to_all(leaving, "comp", split_axis=0, concat_axis=0, tiled=True)
    remapped = jnp.take(arrived.reshape(-1, arrived.shape[2]), ocean_from, axis=0)
    wind_east = remapped[:, 0]
    wind_north = remapped[:, LEV]
    air_temp = remapped[:, 2 * LEV]
    humidity = remapped[:, 3 * LEV]
    speed = jnp.sqrt(wind_east * wind_east + wind_north * wind_north + 1.0)
    saturated = 0.5 * jnp.exp(0.2 * surface_temp)
    fluxes = jnp.stack(
        [
            0.6 * speed * (air_temp - surface_temp),
            0.6 * speed * (humidity - saturated),
            0.6 * speed * (wind_east - ocean_current[0]),
            0.6 * speed * (wind_north - ocean_current[1]),
        ]
    )
    return (remapped, fluxes)


def solution(mesh):
    return jax.shard_map(
        shards,
        mesh=mesh,
        in_specs=(
            P("comp", None),
            P("comp", None, None),
            P("comp", None),
            P("comp", None),
            P("comp", None),
            P("comp"),
            P("comp"),
            P(None, "comp"),
        ),
        out_specs=(P("comp", None), P(None, "comp")),
        check_vma=False,
    )
```

profile of v0, /device:TPU:1, one launch (start us, length us, event | category | flops | bytes accessed | tf_op | source)
XLA Modules:
  0.0 138.4 jit_solution(17622480217923119046)
XLA Ops:
  0.6 0.0 copy-start
  0.6 0.8 compare_select_fusion.2
  1.5 0.7 compare_and_fusion.2
  2.2 1.1 copy.27
  3.3 0.1 copy.26
  3.4 0.1 reshape.80
  3.5 0.1 copy.25
  3.7 4.8 %gather_fusion = f32[1024,320]{1,0:T(8,128)} fusion(f32[256,320]{1,0:T(8,128)S(1)} %copy.27, s32[1024]{0:T(1024)S(1)} %broadcast_clamp_fusion.2), kind=kCustom, calls=%fused_computation | custom fusion | bytes 2625536 | tf_op jit(solution)/shard_map/jit(_take)/gather | solution.py:15
  8.4 2.8 %bitcast_select_fusion = f32[128,8,320]{2,1,0:T(8,128)} fusion(f32[1024,320]{1,0:T(8,128)} %gather_fusion, pred[128,8]{1,0:T(8,128)(4,1)S(1)} %copy.25), kind=kLoop, calls=%fused_computation.6 | loop fusion | flops 327680 | bytes 2622464 | tf_op jit(solution)/shard_map/jit(_take)/select_n | solution.py:15
  11.2 0.0 copy-start.3
  11.2 0.0 copy-start.2
  11.2 11.9 %all-to-all-start = ((f32[128,8,320]{2,1,0:T(8,128)}), f32[128,8,320]{2,1,0:T(8,128)}, u32[]{:S(2)}, u32[]{:S(2)}) async-start(f32[128,8,320]{2,1,0:T(8,128)} %bitcast_select_fusion), calls=%async_computation | async-start | bytes 3145728 | tf_op jit(solution)/shard_map/all_to_all | solution.py:16
  23.1 0.0 copy-done.3
  23.1 0.0 copy-done.2
  23.2 0.1 copy.30
  23.3 0.1 reshape.96
  23.4 0.1 copy.24
  23.5 24.2 %all-to-all-done = f32[128,8,320]{2,1,0:T(8,128)} async-done(((f32[128,8,320]{2,1,0:T(8,128)}), f32[128,8,320]{2,1,0:T(8,128)}, u32[]{:S(2)}, u32[]{:S(2)}) %all-to-all-start) | async-done | bytes 1310752 | tf_op jit(solution)/shard_map/all_to_all | solution.py:16
  47.7 10.5 %gather_fusion.1 = f32[2048,320]{1,0:T(8,128)} fusion(f32[1024,320]{1,0:T(8,128)} %bitcast.1, s32[2048]{0:T(1024)S(1)} %broadcast_clamp_fusion.1), kind=kCustom, calls=%fused_computation.1 | custom fusion | bytes 5251072 | tf_op jit(solution)/shard_map/jit(_take)/gather | solution.py:19
  58.2 3.4 %copy.28 = f32[4,512,320]{1,2,0:T(8,128)} copy(f32[4,512,320]{2,1,0:T(8,128)} %bitcast.42) | data formatting | bytes 5242880 | tf_op jit(solution)/shard_map/jit(_take)/gather | solution.py:19
  61.6 0.0 copy-done
  61.6 4.3 %fusion.2 = f32[4,256,320]{1,2,0:T(8,128)S(1)} fusion(f32[4,256,512]{2,1,0:T(8,128)S(1)} %copy-done, f32[4,512,320]{1,2,0:T(8,128)} %copy.28, pred[4,512]{1,0:T(4,128)(4,1)S(1)} %compare_and_fusion), kind=kOutput, calls=%fused_computation.8 | convolution fusion | flops 2013921280 | bytes 6031360 | tf_op jit(solution)/shard_map/bos,bsw->bow/dot_general | solution.py:20
  66.0 1.6 %copy.33 = f32[4,256,320]{2,1,0:T(8,128)} copy(f32[4,256,320]{1,2,0:T(8,128)S(1)} %fusion.2) | data formatting | bytes 2621440 | tf_op jit(solution)/shard_map/reshape | solution.py:27
  67.6 10.5 %gather_fusion.2 = f32[2048,320]{1,0:T(8,128)} fusion(f32[1024,320]{1,0:T(8,128)} %bitcast.40, s32[2048]{0:T(1024)S(1)} %broadcast_clamp_fusion), kind=kCustom, calls=%fused_computation.2 | custom fusion | bytes 5251072 | tf_op jit(solution)/shard_map/jit(_take)/gather | solution.py:28
  78.1 3.3 %broadcast_select_fusion = f32[128,16,320]{2,1,0:T(8,128)} fusion(f32[128,16,320]{2,1,0:T(8,128)} %bitcast.41, pred[128,16]{1,0:T(8,128)(4,1)S(1)} %copy.24), kind=kLoop, calls=%fused_computation.7 | loop fusion | flops 655360 | bytes 5244928 | tf_op jit(solution)/shard_map/jit(_take)/select_n | solution.py:28
  81.4 0.0 copy-start.4
  81.4 5.5 %all-to-all-start.1 = ((f32[128,16,320]{2,1,0:T(8,128)}), f32[128,16,320]{2,1,0:T(8,128)}, u32[]{:S(2)}, u32[]{:S(2)}) async-start(f32[128,16,320]{2,1,0:T(8,128)} %broadcast_select_fusion), calls=%async_computation.1 | async-start | bytes 6291456 | tf_op jit(solution)/shard_map/all_to_all | solution.py:29
  86.9 0.0 copy-done.4
  86.9 41.3 %all-to-all-done.1 = f32[128,16,320]{2,1,0:T(8,128)} async-done(((f32[128,16,320]{2,1,0:T(8,128)}), f32[128,16,320]{2,1,0:T(8,128)}, u32[]{:S(2)}, u32[]{:S(2)}) %all-to-all-start.1) | async-done | bytes 2621472 | tf_op jit(solution)/shard_map/all_to_all | solution.py:29
  128.2 6.9 %gather_fusion.3 = f32[1024,320]{1,0:T(8,128)} fusion(f32[2048,320]{1,0:T(8,128)} %bitcast.6, s32[1024]{0:T(1024)S(1)} %fusion.12), kind=kCustom, calls=%fused_computation.3 | custom fusion | bytes 2625536 | tf_op jit(solution)/shard_map/jit(_take)/gather | solution.py:30
  135.1 1.9 %copy.32 = f32[1024,320]{0,1:T(8,128)S(1)} copy(f32[1024,320]{1,0:T(8,128)} %gather_fusion.3) | data formatting | bytes 2621440 | tf_op jit(solution)/shard_map/jit(_take)/gather | solution.py:30
  137.0 0.0 copy-start.5
  137.0 0.0 copy-start.6
  137.0 0.2 broadcast_select_fusion.1
  137.2 0.0 copy-start.1
  137.2 0.5 copy-done.5
  137.7 0.0 copy-done.6
  137.8 0.6 pad_maximum_fusion
  138.4 0.0 copy-done.1
  (14 shorter events, 0.1 us)
Async XLA Ops:
  0.6 61.0 %copy-start = (f32[4,256,512]{2,1,0:T(8,128)S(1)}, f32[4,256,512]{2,1,0:T(8,128)}, u32[]{:S(2)}) copy-start(f32[4,256,512]{2,1,0:T(8,128)} %param.9) | copy-start | bytes 6291460
  11.2 11.9 %copy-start.3 = (s32[4,512]{1,0:T(4,128)S(1)}, s32[4,512]{1,0:T(4,128)}, u32[]{:S(2)}) copy-start(s32[4,512]{1,0:T(4,128)} %param.10) | copy-start | bytes 24580
  11.2 11.9 %copy-start.2 = (s32[128,16]{0,1:T(8,128)S(1)}, s32[128,16]{0,1:T(8,128)}, u32[]{:S(2)}) copy-start(s32[128,16]{0,1:T(8,128)} %param.12) | copy-start | bytes 24580
  11.2 36.5 %all-to-all-start = ((f32[128,8,320]{2,1,0:T(8,128)}), f32[128,8,320]{2,1,0:T(8,128)}, u32[]{:S(2)}, u32[]{:S(2)}) async-start(f32[128,8,320]{2,1,0:T(8,128)} %bitcast_select_fusion), calls=%async_computation | async-start | bytes 3145728 | tf_op jit(solution)/shard_map/all_to_all | solution.py:16
  81.4 5.5 %copy-start.4 = (s32[1024]{0:T(1024)S(1)}, s32[1024]{0:T(1024)}, u32[]{:S(2)}) copy-start(s32[1024]{0:T(1024)} %param.13) | copy-start | bytes 12292
  81.4 46.9 %all-to-all-start.1 = ((f32[128,16,320]{2,1,0:T(8,128)}), f32[128,16,320]{2,1,0:T(8,128)}, u32[]{:S(2)}, u32[]{:S(2)}) async-start(f32[128,16,320]{2,1,0:T(8,128)} %broadcast_select_fusion), calls=%async_computation.1 | async-start | bytes 6291456 | tf_op jit(solution)/shard_map/all_to_all | solution.py:29
  137.0 0.7 copy-start.5
  137.0 0.7 copy-start.6
  137.2 1.2 copy-start.1
where the time goes:
time: 139 us; the launch traced here: 138 us
  waiting for transfers between devices  65.5 us (47%)
  local copies, waits for them, and re-layouts  41.8 us (30%)
  starting transfers between devices  17.4 us (13%)
  other arithmetic  8.5 us (6%)
  matrix products  4.32 us (3%)
    all_to_all x1, waiting for transfers between devices, shards(): lax.all_to_all(leaving, 'comp', split_axis=0, concat_axis=0, tiled=True)  41.3 us
    all_to_all x1, waiting for transfers between devices, shards(): lax.all_to_all(outgoing, 'comp', split_axis=0, concat_axis=0, tiled=True)  24.2 us
    gather x2, local copies, waits for them, and re-layouts, shards(): picked = jnp.take(flat_rows, block_src, axis=0)  13.9 us
    all_to_all x1, starting transfers between devices, shards(): lax.all_to_all(outgoing, 'comp', split_axis=0, concat_axis=0, tiled=True)  11.9 us
    gather x1, local copies, waits for them, and re-layouts, shards(): leaving = jnp.take(coupled, coupler_send, axis=0)  10.5 us
    gather x2, local copies, waits for them, and re-layouts, shards(): jnp.take(arrived.reshape(-1, arrived.shape[2]), ocean_from, axis=0)  8.73 us
    all_to_all x1, starting transfers between devices, shards(): lax.all_to_all(leaving, 'comp', split_axis=0, concat_axis=0, tiled=True)  5.51 us
    gather x1, local copies, waits for them, and re-layouts, shards(): outgoing = jnp.take(src_fields, send_src, axis=0)  4.77 us
  transfers between devices with their start and end apart: 2, of which 2 were waited for; matrix products, arithmetic and copies ran while one was open for 0% of the time, Pallas kernels for 0%

commit v1 on v0

v1 whole, which is shorter than its diff:
```python
import jax
import jax.numpy as jnp
from jax import lax
from jax.experimental import pallas as pl
from jax.experimental.pallas import tpu as pltpu
from jax.sharding import PartitionSpec as P

LEV = 8
LANES = 128
HALF = LANES // 2
BF16 = jnp.bfloat16
F32 = jnp.float32


def split(x):
    high = x.astype(BF16)
    low = (x - high.astype(F32)).astype(BF16)
    return high, low


def dot(a, b, dims):
    return lax.dot_general(a, b, (dims, ((), ())), preferred_element_type=F32)


def gather_kernel(send_ref, src_ref, out_ref):
    slots, devices = send_ref.shape
    rows = src_ref.shape[1]
    high, low = split(src_ref[...])
    picks = send_ref[...].T
    stride = slots * 5 // 2
    tails = []
    for k in range(slots):
        hot = jnp.where(
            lax.broadcasted_iota(jnp.int32, (devices, rows), 1) == picks[:, k : k + 1], 1.0, 0.0
        ).astype(BF16)
        taken = dot(hot, high, ((1,), (1,))) + dot(hot, low, ((1,), (1,)))
        out_ref[pl.ds(k, devices, stride=stride), :] = taken[:, :LANES]
        out_ref[pl.ds(slots + k, devices, stride=stride), :] = taken[:, LANES : 2 * LANES]
        tails.append(taken[:, 2 * LANES :])
    for k in range(slots // 2):
        both = jnp.concatenate([tails[k], tails[k + slots // 2]], axis=1)
        out_ref[pl.ds(2 * slots + k, devices, stride=stride), :] = both


def spread_kernel(slots, src_ref, weights_ref, high_ref, low_ref):
    blocks, block_rows, block_cols = weights_ref.shape
    total = high_ref.shape[1]
    senders = total // slots
    for b in range(blocks):
        slot = src_ref[b : b + 1, :]
        column = (slot % slots) * senders + slot // slots
        hot = jnp.where(
            lax.broadcasted_iota(jnp.int32, (total, block_cols), 0) == column, 1.0, 0.0
        ).astype(BF16)
        high, low = split(weights_ref[b])
        summed = dot(high, hot, ((1,), (1,))) + dot(low, hot, ((1,), (1,)))
        high, low = split(summed)
        high_ref[pl.ds(b * block_rows, block_rows), :] = high
        low_ref[pl.ds(b * block_rows, block_rows), :] = low


def couple_kernel(slots, send_ref, high_ref, low_ref, recv_ref, out_ref, first_ref, second_ref, tail_ref):
    senders = high_ref.shape[1] // slots
    stride = slots * 5 // 2
    heads, tails = [], []
    for k in range(slots):
        heads.append(
            jnp.concatenate(
                [
                    recv_ref[pl.ds(k, senders, stride=stride), :],
                    recv_ref[pl.ds(slots + k, senders, stride=stride), :],
                ],
                axis=1,
            )
        )
    for k in range(slots // 2):
        both = recv_ref[pl.ds(2 * slots + k, senders, stride=stride), :]
        tails.append(both)
    lane = lax.broadcasted_iota(jnp.int32, (senders, LANES), 1)
    lower = [jnp.where(lane < HALF, t, pltpu.roll(t, HALF, 1)) for t in tails]
    upper = [jnp.where(lane < HALF, pltpu.roll(t, HALF, 1), t) for t in tails]
    head_high, head_low = split(jnp.concatenate(heads, axis=0))
    tail_high, tail_low = split(jnp.concatenate(lower + upper, axis=0))
    high, low = high_ref[...], low_ref[...]
    contract = ((1,), (0,))
    head = dot(high, head_high, contract) + dot(high, head_low, contract) + dot(low, head_high, contract)
    first_ref[...] = head[:, :LANES]
    second_ref[...] = head[:, LANES:]
    tail_ref[...] = dot(high, tail_high, contract) + dot(high, tail_low, contract) + dot(low, tail_high, contract)

    oceans = send_ref.shape[1]
    slots2 = send_ref.shape[0]
    wide = slots2 * 5 // 2
    left = lax.broadcasted_iota(jnp.int32, (1, LANES), 1) < HALF

    def one_ocean(o, carry):
        base = pl.multiple_of(o * wide, 8)
        rows = [send_ref[k, o] for k in range(slots2)]
        for k in range(slots2):
            out_ref[pl.ds(base + k, 1), :] = first_ref[pl.ds(rows[k], 1), :]
            out_ref[pl.ds(base + slots2 + k, 1), :] = second_ref[pl.ds(rows[k], 1), :]
        for k in range(slots2 // 2):
            out_ref[pl.ds(base + 2 * slots2 + k, 1), :] = jnp.where(
                left, tail_ref[pl.ds(rows[k], 1), :], tail_ref[pl.ds(rows[k + slots2 // 2], 1), :]
            )
        return carry

    lax.fori_loop(0, oceans, one_ocean, 0)


def place_kernel(slots2, from_ref, lane_ref, temp_ref, current_ref, arrived_ref, out_ref, flux_ref, first_ref, second_ref, tail_ref):
    cells = out_ref.shape[1]
    wide = slots2 * 5 // 2
    half = slots2 // 2
    unroll = 16

    def some(step, carry):
        base = pl.multiple_of(step * unroll, unroll)
        for j in range(unroll):
            slot = from_ref[base + j]
            row = (slot // slots2) * wide
            k = slot % slots2
            first_ref[pl.ds(base + j, 1), :] = arrived_ref[pl.ds(row + k, 1), :]
            second_ref[pl.ds(base + j, 1), :] = arrived_ref[pl.ds(row + slots2 + k, 1), :]
            tail_ref[pl.ds(base + j, 1), :] = arrived_ref[pl.ds(row + 2 * slots2 + k % half, 1), :]
        return carry

    lax.fori_loop(0, cells // unroll, some, 0)
    first = first_ref[...].T
    out_ref[:LANES, :] = first
    out_ref[LANES : 2 * LANES, :] = second_ref[...].T
    tail = tail_ref[...].T
    lower = lane_ref[...] % slots2 < half
    out_ref[2 * LANES :, :] = jnp.where(lower, tail[:HALF], tail[HALF:])
    wind_east = first[0:1]
    wind_north = first[LEV : LEV + 1]
    air_temp = first[2 * LEV : 2 * LEV + 1]
    humidity = first[3 * LEV : 3 * LEV + 1]
    surface = temp_ref[...]
    scale = 0.6 * jnp.sqrt(wind_east * wind_east + wind_north * wind_north + 1.0)
    flux_ref[0:1, :] = scale * (air_temp - surface)
    flux_ref[1:2, :] = scale * (humidity - 0.5 * jnp.exp(0.2 * surface))
    flux_ref[2:3, :] = scale * (wind_east - current_ref[0:1, :])
    flux_ref[3:4, :] = scale * (wind_north - current_ref[1:2, :])


def vmem():
    return pl.BlockSpec(memory_space=pltpu.VMEM)


def smem():
    return pl.BlockSpec(memory_space=pltpu.SMEM)


def params():
    return pltpu.CompilerParams(vmem_limit_bytes=48 * 1024 * 1024)


def exchange(flat, devices):
    rows = flat.shape[0] // devices
    shaped = flat.reshape(devices, rows // 4, 4, LANES)
    moved = lax.all_to_all(shaped, "comp", split_axis=0, concat_axis=0, tiled=True)
    return moved.reshape(flat.shape)


def shards(
    src_fields, weights, block_src, send_src, coupler_send, ocean_from, surface_temp, ocean_current
):
    devices = lax.axis_size("comp")
    slots, slots2 = send_src.shape[1], coupler_send.shape[1]
    blocks, block_rows, block_cols = weights.shape
    columns = src_fields.shape[1]
    cells = ocean_from.shape[0]
    total = devices * slots
    coupled = blocks * block_rows

    outgoing = pl.pallas_call(
        gather_kernel,
        out_shape=jax.ShapeDtypeStruct((devices * slots * 5 // 2, LANES), F32),
        in_specs=[vmem(), vmem()],
        out_specs=vmem(),
        compiler_params=params(),
        name="gather_rows",
    )(send_src.T, src_fields.T)
    received = exchange(outgoing, devices)

    high, low = pl.pallas_call(
        lambda *refs: spread_kernel(slots, *refs),
        out_shape=[jax.ShapeDtypeStruct((coupled, total), BF16)] * 2,
        in_specs=[vmem(), vmem()],
        out_specs=[vmem(), vmem()],
        compiler_params=params(),
        name="spread_weights",
    )(block_src, weights)

    leaving = pl.pallas_call(
        lambda *refs: couple_kernel(slots, *refs),
        out_shape=jax.ShapeDtypeStruct((devices * slots2 * 5 // 2, LANES), F32),
        in_specs=[smem(), vmem(), vmem(), vmem()],
        out_specs=vmem(),
        scratch_shapes=[pltpu.VMEM((coupled, LANES), F32)] * 3,
        compiler_params=params(),
        name="couple",
    )(coupler_send.T, high, low, received)
    arrived = exchange(leaving, devices)

    remapped, fluxes = pl.pallas_call(
        lambda *refs: place_kernel(slots2, *refs),
        out_shape=[jax.ShapeDtypeStruct((columns, cells), F32), jax.ShapeDtypeStruct((4, cells), F32)],
        in_specs=[smem(), vmem(), vmem(), vmem(), vmem()],
        out_specs=[vmem(), vmem()],
        scratch_shapes=[pltpu.VMEM((cells, LANES), F32)] * 3,
        compiler_params=params(),
        name="place",
    )(ocean_from, ocean_from[None], surface_temp[None], ocean_current, arrived)
    return (remapped.T, fluxes)


def solution(mesh):
    return jax.shard_map(
        shards,
        mesh=mesh,
        in_specs=(
            P("comp", None),
            P("comp", None, None),
            P("comp", None),
            P("comp", None),
            P("comp", None),
            P("comp"),
            P("comp"),
            P(None, "comp"),
        ),
        out_specs=(P("comp", None), P(None, "comp")),
        check_vma=False,
    )
```

time: 139 us -> 103 us (0.74)
  waiting for transfers between devices: 65.5 us -> 16.1 us
  blocking collectives: 0 us -> 40.8 us
  local copies, waits for them, and re-layouts: 41.8 us -> 4.59 us
  Pallas kernels: 0 us -> 29 us
  other arithmetic: 8.5 us -> 0 us
  starting transfers between devices: 17.4 us -> 11.5 us
  matrix products: 4.32 us -> 0 us
    all_to_all x2 -> x1, waiting for transfers between devices: 65.5 us -> 16.1 us  [exchange(): lax.all_to_all(shaped, 'comp', split_axis=0, concat_axis=0, tiled=True)]
    all_to_all x0 -> x1, blocking collectives: none -> 40.8 us  [exchange(): lax.all_to_all(shaped, 'comp', split_axis=0, concat_axis=0, tiled=True)]
    gather x6 -> x0, local copies, waits for them, and re-layouts: 37.9 us -> none  [the longest x2 13.9 us: shards(): picked = jnp.take(flat_rows, block_src, axis=0)]
    pallas_call x0 -> x4, Pallas kernels: none -> 29 us  [the longest x1 12 us: shards(): pl.pallas_call(lambda *refs: place_kernel(slots2, *refs), out_shape=[jax....]
    select_n x5 -> x0, other arithmetic: 7.06 us -> none  [the longest x2 3.61 us: shards(): outgoing = jnp.take(src_fields, send_src, axis=0)]
    all_to_all x2 -> x1, starting transfers between devices: 17.4 us -> 11.5 us  [exchange(): lax.all_to_all(shaped, 'comp', split_axis=0, concat_axis=0, tiled=True)]
    dot_general x1 -> x0, matrix products: 4.32 us -> none  [shards(): jnp.einsum('bos,bsw->bow', weights, picked, precision=lax.Precision.HIGHE...]
    unnamed x16 -> x18, local copies, waits for them, and re-layouts: 1.64 us -> 4.59 us
  transfers between devices with their start and end apart: 2 -> 1, of which waited for: 2 -> 1; matrix products, arithmetic and copies ran while one was open for 0% -> 0% of each run, Pallas kernels for 0% -> 5%
where the time goes in v1:
time: 103 us
  blocking collectives  40.8 us (40%)
  Pallas kernels  29 us (28%)
  waiting for transfers between devices  16.1 us (16%)
  starting transfers between devices  11.5 us (11%)
  local copies, waits for them, and re-layouts  4.59 us (4%)
    all_to_all x1, blocking collectives, exchange(): lax.all_to_all(shaped, 'comp', split_axis=0, concat_axis=0, tiled=True)  40.8 us
    all_to_all x1, waiting for transfers between devices, exchange(): lax.all_to_all(shaped, 'comp', split_axis=0, concat_axis=0, tiled=True)  16.1 us
    pallas_call x1, Pallas kernels, shards(): pl.pallas_call(lambda *refs: place_kernel(slots2, *refs), out_shape=[jax....  12 us
    all_to_all x1, starting transfers between devices, exchange(): lax.all_to_all(shaped, 'comp', split_axis=0, concat_axis=0, tiled=True)  11.5 us
    pallas_call x1, Pallas kernels, shards(): pl.pallas_call(lambda *refs: couple_kernel(slots, *refs), out_shape=jax.S...  10 us
    pallas_call x1, Pallas kernels, shards(): pl.pallas_call(lambda *refs: spread_kernel(slots, *refs), out_shape=[jax....  4.75 us
    unnamed x18, local copies, waits for them, and re-layouts  4.59 us
    pallas_call x1, Pallas kernels, shards(): pl.pallas_call(gather_kernel, out_shape=jax.ShapeDtypeStruct((devices * s...  2.28 us
  transfers between devices with their start and end apart: 1, of which 1 were waited for; matrix products, arithmetic and copies ran while one was open for 0% of the time, Pallas kernels for 5%

profile of v1, /device:TPU:1, one launch (start us, length us, event | category | flops | bytes accessed | tf_op | source)
XLA Modules:
  0.0 102.7 jit_solution(15707255886756403047)
XLA Ops:
  0.6 0.0 copy-start.2
  0.6 1.0 copy-done.2
  1.6 0.0 copy-start.7
  1.6 0.7 copy-done.7
  2.3 0.0 copy-start.4
  2.3 2.3 %gather_rows.1 = f32[2560,128]{1,0:T(8,128)} custom-call(s32[8,128]{1,0:T(8,128)S(1)} %bitcast.15, f32[320,256]{1,0:T(8,128)S(1)} %bitcast.12), custom_call_target="tpu_custom_call" | custom-call | tf_op jit(solution)/shard_map/gather_rows/pallas_call | solution.py:177
  4.6 0.0 copy-start.5
  4.6 11.5 %all-to-all-start = ((f32[128,5,4,128]{3,2,1,0:T(4,128)}), f32[128,5,4,128]{3,2,1,0:T(4,128)S(1)}, u32[]{:S(2)}, u32[]{:S(2)}) async-start(f32[128,5,4,128]{3,2,1,0:T(4,128)} %bitcast.5), calls=%async_computation | async-start | bytes 2621440 | tf_op jit(solution)/shard_map/all_to_all | solution.py:162
  16.1 0.0 copy-done.4
  16.1 4.7 %spread_weights.1 = (bf16[1024,1024]{1,0:T(8,128)(2,1)S(1)}, bf16[1024,1024]{1,0:T(8,128)(2,1)S(1)}) custom-call(s32[4,512]{1,0:T(4,128)S(1)} %copy-done.4, f32[4,256,512]{2,1,0:T(8,128)} %refs_1_.1), custom_call_target="tpu_custom_call" | custom-call | tf_op jit(solution)/shard_map/spread_weights/pallas_call | solution.py:187
  20.8 0.0 copy-start
  20.9 1.3 %copy-done = bf16[1024,1024]{1,0:T(8,128)(2,1)} copy-done((bf16[1024,1024]{1,0:T(8,128)(2,1)}, bf16[1024,1024]{1,0:T(8,128)(2,1)S(1)}, u32[]{:S(2)}) %copy-start) | copy-done | bytes 2097176
  22.2 16.1 %all-to-all-done = f32[128,5,4,128]{3,2,1,0:T(4,128)S(1)} async-done(((f32[128,5,4,128]{3,2,1,0:T(4,128)}), f32[128,5,4,128]{3,2,1,0:T(4,128)S(1)}, u32[]{:S(2)}, u32[]{:S(2)}) %all-to-all-start) | async-done | bytes 1310752 | tf_op jit(solution)/shard_map/all_to_all | solution.py:162
  38.2 0.0 copy-done.5
  38.2 0.0 copy-start.1
  38.2 1.6 %copy-done.1 = bf16[1024,1024]{1,0:T(8,128)(2,1)S(1)} copy-done((bf16[1024,1024]{1,0:T(8,128)(2,1)S(1)}, bf16[1024,1024]{1,0:T(8,128)(2,1)}, u32[]{:S(2)}) %copy-start.1) | copy-done | bytes 2097176
  39.8 10.0 %couple.1 = f32[5120,128]{1,0:T(8,128)} custom-call(s32[16,128]{1,0:T(8,128)S(1)} %bitcast.14, bf16[1024,1024]{1,0:T(8,128)(2,1)S(1)} %get-tuple-element.6.refs_1_, bf16[1024,1024]{1,0:T(8,128)(2,1)S(1)} %copy-done.1, f32[2560,128]{1,0:T(8,128)S(1)} %bitcast.11), custom_call_target="tpu_custom_call" | custom-call | tf_op jit(solution)/shard_map/couple/pallas_call | solution.py:196
  49.9 0.0 copy-start.3
  49.9 0.0 copy-start.6
  49.9 0.0 copy-start.8
  49.9 40.8 %all_to_all.10 = f32[128,10,4,128]{3,2,1,0:T(4,128)S(1)} all-to-all(f32[128,10,4,128]{3,2,1,0:T(4,128)} %bitcast.17), channel_id=1, replica_groups=mesh['comp'=128] {'comp'}, dimensions={0} | all-to-all | bytes 5242880 | tf_op jit(solution)/shard_map/all_to_all | solution.py:162
  90.7 0.0 copy-done.3
  90.7 0.0 copy-done.6
  90.7 0.0 copy-done.8
  90.7 12.0 %place.1 = (f32[320,1024]{1,0:T(8,128)}, f32[4,1024]{1,0:T(4,128)}) custom-call(s32[1024]{0:T(1024)S(1)} %copy-done.3, s32[1,1024]{1,0:T(1,128)S(1)} %bitcast.13, f32[1,1024]{1,0:T(1,128)S(1)} %bitcast.16, f32[2,1024]{1,0:T(2,128)S(1)} %copy-done.6, f32[5120,128]{1,0:T(8,128)S(1)} %bitcast.10), custom_call_target="tpu_custom_call" | custom-call | tf_op jit(solution)/shard_map/place/pallas_call | solution.py:207
Async XLA Ops:
  0.6 1.0 copy-start.2
  1.6 0.7 copy-start.7
  2.3 13.8 %copy-start.4 = (s32[4,512]{1,0:T(4,128)S(1)}, s32[4,512]{1,0:T(4,128)}, u32[]{:S(2)}) copy-start(s32[4,512]{1,0:T(4,128)} %refs_0_.2) | copy-start | bytes 24580
  4.6 33.7 %copy-start.5 = (s32[128,16]{0,1:T(8,128)S(1)}, s32[128,16]{0,1:T(8,128)}, u32[]{:S(2)}) copy-start(s32[128,16]{0,1:T(8,128)} %param.12) | copy-start | bytes 24580
  4.6 33.7 %all-to-all-start = ((f32[128,5,4,128]{3,2,1,0:T(4,128)}), f32[128,5,4,128]{3,2,1,0:T(4,128)S(1)}, u32[]{:S(2)}, u32[]{:S(2)}) async-start(f32[128,5,4,128]{3,2,1,0:T(4,128)} %bitcast.5), calls=%async_computation | async-start | bytes 2621440 | tf_op jit(solution)/shard_map/all_to_all | solution.py:162
  20.8 1.3 %copy-start = (bf16[1024,1024]{1,0:T(8,128)(2,1)}, bf16[1024,1024]{1,0:T(8,128)(2,1)S(1)}, u32[]{:S(2)}) copy-start(bf16[1024,1024]{1,0:T(8,128)(2,1)S(1)} %get-tuple-element.7.refs_2_) | copy-start | bytes 6291460
  38.2 1.6 %copy-start.1 = (bf16[1024,1024]{1,0:T(8,128)(2,1)S(1)}, bf16[1024,1024]{1,0:T(8,128)(2,1)}, u32[]{:S(2)}) copy-start(bf16[1024,1024]{1,0:T(8,128)(2,1)} %copy-done) | copy-start | bytes 6291460
  49.9 40.8 %copy-start.3 = (s32[1024]{0:T(1024)S(1)}, s32[1024]{0:T(1024)}, u32[]{:S(2)}) copy-start(s32[1024]{0:T(1024)} %refs_0_.3) | copy-start | bytes 12292
  49.9 40.8 %copy-start.6 = (f32[2,1024]{1,0:T(2,128)S(1)}, f32[2,1024]{1,0:T(2,128)}, u32[]{:S(2)}) copy-start(f32[2,1024]{1,0:T(2,128)} %refs_3_.1) | copy-start | bytes 24580
  49.9 40.8 %copy-start.8 = (f32[1024]{0:T(1024)S(1)}, f32[1024]{0:T(1024)}, u32[]{:S(2)}) copy-start(f32[1024]{0:T(1024)} %param.14) | copy-start | bytes 12292

commit v2 on v0

v2 whole, which is shorter than its diff:
```python
import jax
import jax.numpy as jnp
from jax import lax
from jax.experimental import pallas as pl
from jax.experimental.pallas import tpu as pltpu
from jax.sharding import PartitionSpec as P

LEV = 8
LANES = 128
HALF = LANES // 2
SUB = 8
BF16 = jnp.bfloat16
F32 = jnp.float32
I32 = jnp.int32
MIB = 1024 * 1024


def split(x):
    high = x.astype(BF16)
    low = (x - high.astype(F32)).astype(BF16)
    return high, low


def dot(a, b, dims):
    return lax.dot_general(a, b, (dims, ((), ())), preferred_element_type=F32)


def iota(shape, dim):
    return lax.broadcasted_iota(I32, shape, dim)


def one_hot(mask):
    return jnp.where(mask, 1.0, 0.0).astype(BF16)


def gather_kernel(send_hbm, src_hbm, out_hbm, send_ref, src_ref, out_ref, in_sems, out_sems):
    slots, devices = send_ref.shape
    columns, rows = src_ref.shape
    pieces = in_sems.shape[0] - 1
    piece = columns // pieces
    send_copy = pltpu.make_async_copy(send_hbm, send_ref, in_sems.at[pieces])
    send_copy.start()
    copies = []
    for i in range(pieces):
        part = pl.ds(i * piece, piece)
        copies.append(pltpu.make_async_copy(src_hbm.at[part], src_ref.at[part], in_sems.at[i]))
        copies[-1].start()
    send_copy.wait()
    picks = send_ref[...].T
    stride = slots * 5 // 2
    groups = out_sems.shape[0]
    each = devices // groups
    hots = []
    for g in range(groups):
        some = picks[g * each : (g + 1) * each]
        hots.append(
            jnp.concatenate(
                [one_hot(iota((each, rows), 1) == some[:, k : k + 1]) for k in range(slots)], axis=0
            )
        )
    for copy in copies:
        copy.wait()
    high, low = split(src_ref[...])
    copies = []
    for g in range(groups):
        taken = dot(hots[g], high, ((1,), (1,))) + dot(hots[g], low, ((1,), (1,)))
        taken = [taken[k * each : (k + 1) * each] for k in range(slots)]
        base = g * each * stride
        for k in range(slots):
            out_ref[pl.ds(base + k, each, stride=stride), :] = taken[k][:, :LANES]
            out_ref[pl.ds(base + slots + k, each, stride=stride), :] = taken[k][:, LANES : 2 * LANES]
        for k in range(slots // 2):
            both = jnp.concatenate(
                [taken[k][:, 2 * LANES :], taken[k + slots // 2][:, 2 * LANES :]], axis=1
            )
            out_ref[pl.ds(base + 2 * slots + k, each, stride=stride), :] = both
        part = pl.ds(base, each * stride)
        copies.append(pltpu.make_async_copy(out_ref.at[part], out_hbm.at[part], out_sems.at[g]))
        copies[-1].start()
    for copy in copies:
        copy.wait()


def spread_kernel(slots, src_ref, weights_ref, send_ref, spread_ref, place_ref):
    blocks, block_rows, block_cols = weights_ref.shape
    total = spread_ref.shape[2]
    senders = total // slots
    for b in range(blocks):
        slot = src_ref[b : b + 1, :]
        column = (slot % slots) * senders + slot // slots
        hot = one_hot(iota((total, block_cols), 0) == column)
        high, low = split(weights_ref[b])
        summed = dot(high, hot, ((1,), (1,))) + dot(low, hot, ((1,), (1,)))
        high, low = split(summed)
        spread_ref[0, pl.ds(b * block_rows, block_rows), :] = high
        spread_ref[1, pl.ds(b * block_rows, block_rows), :] = low

    slots2, oceans = send_ref.shape
    coupled = blocks * block_rows
    send = send_ref[...]
    ocean, position = jnp.zeros((SUB, coupled), F32), jnp.zeros((SUB, coupled), F32)
    for k in range(slots2):
        hot = one_hot(iota((coupled, oceans), 0) == send[k : k + 1])
        ocean += dot(iota((SUB, oceans), 1).astype(BF16), hot, ((1,), (1,)))
        position += dot(jnp.full((SUB, oceans), k, BF16), hot, ((1,), (1,)))
    real = iota((1, coupled), 1) > 0
    ocean = jnp.where(real, ocean[:1].astype(I32), 0)
    position = jnp.where(real, position[:1].astype(I32), 0)
    half = slots2 // 2
    place_ref[0:1, :] = ocean * (slots2 * 5 // 2) + position
    place_ref[1:2, :] = (position // half) * (oceans * half) + ocean * half + position % half


def couple_kernel(
    slots, slots2, place_any, spread_hbm, recv_ref, out_hbm,
    place_ref, spread_ref, head_high_ref, head_low_ref, out_ref, tail_ref, block_ref, place_sem, spread_sems, out_sems,
):
    place_copy = pltpu.make_async_copy(place_any, place_ref, place_sem)
    place_copy.start()
    _, coupled, total = spread_ref.shape
    blocks = block_ref.shape[0]
    each = coupled // blocks
    spread_copies = []
    for i in range(blocks):
        rows = pl.ds(i * each, each)
        spread_copies.append(
            pltpu.make_async_copy(spread_hbm.at[:, rows], spread_ref.at[:, rows], spread_sems.at[i])
        )
        spread_copies[-1].start()
    senders = total // slots
    stride = slots * 5 // 2
    left = iota((senders, LANES), 1) < HALF
    for k in range(slots):
        rows = pl.ds(k * senders, senders)
        first = recv_ref[pl.ds(k, senders, stride=stride), :]
        second = recv_ref[pl.ds(slots + k, senders, stride=stride), :]
        both = recv_ref[pl.ds(2 * slots + k % (slots // 2), senders, stride=stride), :]
        turned = pltpu.roll(both, HALF, 1)
        third = jnp.where(left, both, turned) if k < slots // 2 else jnp.where(left, turned, both)
        for i, part in enumerate((first, second, third)):
            high, low = split(part)
            head_high_ref[rows, i * LANES : (i + 1) * LANES] = high
            head_low_ref[rows, i * LANES : (i + 1) * LANES] = low
    place_copy.wait()

    wide = slots2 * 5 // 2
    half = slots2 // 2
    oceans = out_ref.shape[0] // wide
    contract = ((1,), (0,))

    def product(i):
        spread_copies[i].wait()
        rows = pl.ds(i * each, each)
        high, low = spread_ref[0, rows], spread_ref[1, rows]
        block_ref[i] = (
            dot(high, head_high_ref[...], contract)
            + dot(high, head_low_ref[...], contract)
            + dot(low, head_high_ref[...], contract)
        )

    def fill(zero):
        first = jnp.broadcast_to(zero[:, :LANES], (slots2, LANES))
        second = jnp.broadcast_to(zero[:, LANES : 2 * LANES], (slots2, LANES))
        third = jnp.broadcast_to(zero[:, 2 * LANES :], (slots2, LANES))

        def step(o, carry):
            base = pl.multiple_of(o * wide, SUB)
            out_ref[pl.ds(base, slots2), :] = first
            out_ref[pl.ds(base + slots2, slots2), :] = second
            tail_ref[pl.ds(pl.multiple_of(o * slots2, slots2), slots2), :] = third
            return carry

        lax.fori_loop(0, oceans, step, 0, unroll=8)

    def scatter(i):
        group = 8
        for base in range(0, each, group):
            rows = range(base, base + group)
            heads = [place_ref[0, i * each + j] for j in rows]
            tails = [place_ref[1, i * each + j] for j in rows]
            values = [[block_ref[i, j : j + 1, c * LANES : (c + 1) * LANES] for c in range(3)] for j in rows]
            for head, tail, value in zip(heads, tails, values):
                out_ref[pl.ds(head, 1), :] = value[0]
                out_ref[pl.ds(head + slots2, 1), :] = value[1]
                tail_ref[pl.ds(tail, 1), :] = value[2]

    product(0)
    fill(block_ref[0, 0:1, :])
    for i in range(1, blocks):
        product(i)
        scatter(i - 1)
    scatter(blocks - 1)

    pieces = out_sems.shape[0]
    some = oceans // pieces
    left = iota((half, LANES), 1) < HALF
    copies = []
    for q in range(pieces):

        def merge(step, carry):
            o = q * some + step
            near = tail_ref[pl.ds(pl.multiple_of(o * half, half), half), :]
            far = tail_ref[pl.ds(pl.multiple_of(oceans * half + o * half, half), half), :]
            out_ref[pl.ds(pl.multiple_of(o * wide + 2 * slots2, SUB), half), :] = jnp.where(left, near, far)
            return carry

        lax.fori_loop(0, some, merge, 0, unroll=8)
        part = pl.ds(q * some * wide, some * wide)
        copies.append(pltpu.make_async_copy(out_ref.at[part], out_hbm.at[part], out_sems.at[q]))
        copies[-1].start()
    for copy in copies:
        copy.wait()


def place_kernel(
    slots2, head_ref, tail_ref, lower_ref, temp_ref, current_ref, arrived_ref, out_hbm, flux_ref, out_ref, sems,
):
    blocks = sems.shape[0]
    columns = out_ref.shape[1]
    row = iota((SUB, LANES), 0)

    def pick(slots):
        value = arrived_ref[pl.ds(slots[0], SUB, stride=0), :]
        for i in range(1, SUB):
            value = jnp.where(row == i, arrived_ref[pl.ds(slots[i], SUB, stride=0), :], value)
        return value

    def block(b):
        base = b * LANES
        if not isinstance(b, int):
            base = pl.multiple_of(base, LANES)
        first, second, third = [], [], []
        for j in range(0, LANES, SUB):
            heads = [head_ref[base + j + i] for i in range(SUB)]
            tails = [tail_ref[base + j + i] for i in range(SUB)]
            first.append(pick(heads))
            second.append(pick([h + slots2 for h in heads]))
            third.append(pick(tails))
        first = jnp.concatenate(first, axis=0).T
        second = jnp.concatenate(second, axis=0).T
        third = jnp.concatenate(third, axis=0).T
        lanes = pl.ds(base, LANES)
        out_ref[b, :LANES, :] = first
        out_ref[b, LANES : 2 * LANES, :] = second
        out_ref[b, 2 * LANES :, :] = jnp.where(lower_ref[:, lanes] > 0, third[:HALF], third[HALF:])
        pltpu.make_async_copy(out_ref.at[b], out_hbm.at[:, lanes], sems.at[b]).start()
        wind_east = first[0:1]
        wind_north = first[LEV : LEV + 1]
        air_temp = first[2 * LEV : 2 * LEV + 1]
        humidity = first[3 * LEV : 3 * LEV + 1]
        surface = temp_ref[:, lanes]
        scale = 0.6 * jnp.sqrt(wind_east * wind_east + wind_north * wind_north + 1.0)
        flux_ref[0:1, lanes] = scale * (air_temp - surface)
        flux_ref[1:2, lanes] = scale * (humidity - 0.5 * jnp.exp(0.2 * surface))
        flux_ref[2:3, lanes] = scale * (wind_east - current_ref[0:1, lanes])
        flux_ref[3:4, lanes] = scale * (wind_north - current_ref[1:2, lanes])

    for b in range(blocks):
        block(b)
    for b in range(blocks):
        pltpu.make_async_copy(out_ref.at[b], out_hbm.at[:, pl.ds(b * LANES, LANES)], sems.at[b]).wait()


def vmem():
    return pl.BlockSpec(memory_space=pltpu.VMEM)


def smem():
    return pl.BlockSpec(memory_space=pltpu.SMEM)


def hbm():
    return pl.BlockSpec(memory_space=pltpu.HBM)


def in_hbm(x):
    return pltpu.with_memory_space_constraint(x, pltpu.HBM)


def params(mib):
    return pltpu.CompilerParams(vmem_limit_bytes=mib * MIB)


def exchange(flat, devices):
    rows = flat.shape[0] // devices
    shaped = flat.reshape(devices, rows // 4, 4, LANES)
    moved = lax.all_to_all(shaped, "comp", split_axis=0, concat_axis=0, tiled=True)
    return moved.reshape(flat.shape)


def shards(
    src_fields, weights, block_src, send_src, coupler_send, ocean_from, surface_temp, ocean_current
):
    devices = lax.axis_size("comp")
    slots, slots2 = send_src.shape[1], coupler_send.shape[1]
    blocks, block_rows, block_cols = weights.shape
    rows, columns = src_fields.shape
    cells = ocean_from.shape[0]
    total = devices * slots
    coupled = blocks * block_rows
    narrow, wide = slots * 5 // 2, slots2 * 5 // 2
    dma = pltpu.SemaphoreType.DMA

    outgoing = pl.pallas_call(
        gather_kernel,
        out_shape=jax.ShapeDtypeStruct((devices * narrow, LANES), F32),
        in_specs=[hbm(), hbm()],
        out_specs=hbm(),
        scratch_shapes=[
            pltpu.VMEM((slots, devices), I32),
            pltpu.VMEM((columns, rows), F32),
            pltpu.VMEM((devices * narrow, LANES), F32),
            dma((5,)),
            dma((4,)),
        ],
        compiler_params=params(16),
        name="gather_rows",
    )(in_hbm(send_src.T), in_hbm(src_fields.T))
    received = exchange(outgoing, devices)

    spread, place = pl.pallas_call(
        lambda *refs: spread_kernel(slots, *refs),
        out_shape=[
            jax.ShapeDtypeStruct((2, coupled, total), BF16),
            jax.ShapeDtypeStruct((2, coupled), I32),
        ],
        in_specs=[vmem(), vmem(), vmem()],
        out_specs=[vmem(), vmem()],
        compiler_params=params(24),
        name="spread_weights",
    )(block_src, weights, coupler_send.T)

    leaving = pl.pallas_call(
        lambda *refs: couple_kernel(slots, slots2, *refs),
        out_shape=jax.ShapeDtypeStruct((devices * wide, LANES), F32),
        in_specs=[vmem(), hbm(), vmem()],
        out_specs=hbm(),
        scratch_shapes=[
            pltpu.SMEM((2, coupled), I32),
            pltpu.VMEM((2, coupled, total), BF16),
            pltpu.VMEM((total, 3 * LANES), BF16),
            pltpu.VMEM((total, 3 * LANES), BF16),
            pltpu.VMEM((devices * wide, LANES), F32),
            pltpu.VMEM((devices * slots2, LANES), F32),
            pltpu.VMEM((4, coupled // 4, 3 * LANES), F32),
            dma(()),
            dma((4,)),
            dma((8,)),
        ],
        compiler_params=params(24),
        name="couple",
    )(place, in_hbm(spread), received)
    arrived = exchange(leaving, devices)

    base = (ocean_from // slots2) * wide
    position = ocean_from % slots2
    half = slots2 // 2
    head = base + position
    tail = base + 2 * slots2 + position % half
    lower = (position < half).astype(I32)[None]
    remapped, fluxes = pl.pallas_call(
        lambda *refs: place_kernel(slots2, *refs),
        out_shape=[jax.ShapeDtypeStruct((columns, cells), F32), jax.ShapeDtypeStruct((4, cells), F32)],
        in_specs=[smem(), smem(), vmem(), vmem(), vmem(), vmem()],
        out_specs=[hbm(), vmem()],
        scratch_shapes=[
            pltpu.VMEM((cells // LANES, columns, LANES), F32),
            dma((cells // LANES,)),
        ],
        compiler_params=params(16),
        name="place",
    )(head, tail, lower, surface_temp[None], ocean_current, arrived)
    return (remapped.T, fluxes)


def solution(mesh):
    return jax.shard_map(
        shards,
        mesh=mesh,
        in_specs=(
            P("comp", None),
            P("comp", None, None),
            P("comp", None),
            P("comp", None),
            P("comp", None),
            P("comp"),
            P("comp"),
            P(None, "comp"),
        ),
        out_specs=(P("comp", None), P(None, "comp")),
        check_vma=False,
    )
```

time: 139 us -> 89.6 us (0.64)
  local copies, waits for them, and re-layouts: 41.8 us -> 1.97 us
  Pallas kernels: 0 us -> 19.9 us
  waiting for transfers between devices: 65.5 us -> 50.9 us
  other arithmetic: 8.5 us -> 0.03 us
  matrix products: 4.32 us -> 0 us
  starting transfers between devices: 17.4 us -> 15.8 us
    gather x6 -> x0, local copies, waits for them, and re-layouts: 37.9 us -> none  [the longest x2 13.9 us: shards(): picked = jnp.take(flat_rows, block_src, axis=0)]
    pallas_call x0 -> x4, Pallas kernels: none -> 19.9 us  [the longest x1 8.28 us: shards(): pl.pallas_call(lambda *refs: couple_kernel(slots, slots2, *refs), out_sha...]
    all_to_all x2, waiting for transfers between devices: 65.5 us -> 50.9 us  [exchange(): lax.all_to_all(shaped, 'comp', split_axis=0, concat_axis=0, tiled=True)]
    select_n x5 -> x0, other arithmetic: 7.06 us -> none  [the longest x2 3.61 us: shards(): outgoing = jnp.take(src_fields, send_src, axis=0)]
    dot_general x1 -> x0, matrix products: 4.32 us -> none  [shards(): jnp.einsum('bos,bsw->bow', weights, picked, precision=lax.Precision.HIGHE...]
    reshape x1 -> x0, local copies, waits for them, and re-layouts: 1.63 us -> none  [shards(): coupled = coupled.reshape(blocks * block_rows, columns)]
    all_to_all x2, starting transfers between devices: 17.4 us -> 15.8 us  [exchange(): lax.all_to_all(shaped, 'comp', split_axis=0, concat_axis=0, tiled=True)]
  transfers between devices with their start and end apart: 2 -> 2, of which waited for: 2 -> 2; matrix products, arithmetic and copies ran while one was open for 0% -> 0% of each run, Pallas kernels for 0% -> 6%
where the time goes in v2:
time: 89.6 us; the launch traced here: 89.3 us
  waiting for transfers between devices  50.9 us (57%)
  Pallas kernels  19.9 us (22%)
  starting transfers between devices  15.8 us (18%)
  local copies, waits for them, and re-layouts  1.97 us (2%)
    all_to_all x2, waiting for transfers between devices, exchange(): lax.all_to_all(shaped, 'comp', split_axis=0, concat_axis=0, tiled=True)  50.9 us
    all_to_all x2, starting transfers between devices, exchange(): lax.all_to_all(shaped, 'comp', split_axis=0, concat_axis=0, tiled=True)  15.8 us
    pallas_call x1, Pallas kernels, shards(): pl.pallas_call(lambda *refs: couple_kernel(slots, slots2, *refs), out_sha...  8.28 us
    pallas_call x1, Pallas kernels, shards(): pl.pallas_call(lambda *refs: spread_kernel(slots, *refs), out_shape=[jax....  5.39 us
    pallas_call x1, Pallas kernels, shards(): pl.pallas_call(lambda *refs: place_kernel(slots2, *refs), out_shape=[jax....  3.42 us
    pallas_call x1, Pallas kernels, shards(): pl.pallas_call(gather_kernel, out_shape=jax.ShapeDtypeStruct((devices * n...  2.76 us
    unnamed x14, local copies, waits for them, and re-layouts  1.97 us
  transfers between devices with their start and end apart: 2, of which 2 were waited for; matrix products, arithmetic and copies ran while one was open for 0% of the time, Pallas kernels for 6%

profile of v2, /device:TPU:1, one launch (start us, length us, event | category | flops | bytes accessed | tf_op | source)
XLA Modules:
  0.0 89.3 jit_solution(7221430378017322899)
XLA Ops:
  0.6 0.0 copy-start.1
  0.6 0.0 copy-start.2
  0.7 0.0 copy-start.3
  0.7 2.8 %gather_rows.1 = f32[2560,128]{1,0:T(8,128)} custom-call(s32[8,128]{1,0:T(8,128)} %bitcast.16, f32[320,256]{1,0:T(8,128)} %bitcast.15), custom_call_target="tpu_custom_call" | custom-call | tf_op jit(solution)/shard_map/gather_rows/pallas_call | solution.py:304
  3.4 11.5 %all-to-all-start = ((f32[128,5,4,128]{3,2,1,0:T(4,128)}), f32[128,5,4,128]{3,2,1,0:T(4,128)S(1)}, u32[]{:S(2)}, u32[]{:S(2)}) async-start(f32[128,5,4,128]{3,2,1,0:T(4,128)} %bitcast.5), calls=%async_computation | async-start | bytes 2621440 | tf_op jit(solution)/shard_map/all_to_all | solution.py:287
  14.9 0.0 copy-done.1
  15.0 0.0 copy-done.2
  15.0 0.0 copy-done.3
  15.0 5.4 %spread_weights.1 = (bf16[2,1024,1024]{2,1,0:T(8,128)(2,1)S(1)}, s32[2,1024]{1,0:T(2,128)S(1)}) custom-call(s32[4,512]{1,0:T(4,128)S(1)} %copy-done.2, f32[4,256,512]{2,1,0:T(8,128)S(1)} %copy-done.1, s32[16,128]{1,0:T(8,128)S(1)} %bitcast.13), custom_call_target="tpu_custom_call" | custom-call | tf_op jit(solution)/shard_map/spread_weights/pallas_call | solution.py:321
  20.4 0.0 copy-start
  20.4 1.9 %copy-done = bf16[2,1024,1024]{2,1,0:T(8,128)(2,1)} copy-done((bf16[2,1024,1024]{2,1,0:T(8,128)(2,1)}, bf16[2,1024,1024]{2,1,0:T(8,128)(2,1)S(1)}, u32[]{:S(2)}) %copy-start) | copy-done | bytes 4194328
  22.3 14.8 %all-to-all-done = f32[128,5,4,128]{3,2,1,0:T(4,128)S(1)} async-done(((f32[128,5,4,128]{3,2,1,0:T(4,128)}), f32[128,5,4,128]{3,2,1,0:T(4,128)S(1)}, u32[]{:S(2)}, u32[]{:S(2)}) %all-to-all-start) | async-done | bytes 1310752 | tf_op jit(solution)/shard_map/all_to_all | solution.py:287
  37.1 8.3 %couple.1 = f32[5120,128]{1,0:T(8,128)} custom-call(s32[2,1024]{1,0:T(2,128)S(1)} %get-tuple-element.6.refs_0_, bf16[2,1024,1024]{2,1,0:T(8,128)(2,1)} %copy-done, f32[2560,128]{1,0:T(8,128)S(1)} %bitcast.11), custom_call_target="tpu_custom_call" | custom-call | tf_op jit(solution)/shard_map/couple/pallas_call | solution.py:333
  45.4 0.0 copy-start.6
  45.4 0.0 copy-start.4
  45.4 0.0 copy-start.5
  45.4 4.3 %all-to-all-start.1 = ((f32[128,10,4,128]{3,2,1,0:T(4,128)}), f32[128,10,4,128]{3,2,1,0:T(4,128)S(1)}, u32[]{:S(2)}, u32[]{:S(2)}) async-start(f32[128,10,4,128]{3,2,1,0:T(4,128)} %bitcast.7), calls=%async_computation.1 | async-start | bytes 5242880 | tf_op jit(solution)/shard_map/all_to_all | solution.py:287
  49.8 0.0 copy-done.6
  49.8 36.1 %all-to-all-done.1 = f32[128,10,4,128]{3,2,1,0:T(4,128)S(1)} async-done(((f32[128,10,4,128]{3,2,1,0:T(4,128)}), f32[128,10,4,128]{3,2,1,0:T(4,128)S(1)}, u32[]{:S(2)}, u32[]{:S(2)}) %all-to-all-start.1) | async-done | bytes 2621472 | tf_op jit(solution)/shard_map/all_to_all | solution.py:287
  85.9 0.0 copy-done.4
  85.9 0.0 copy-done.5
  85.9 3.4 %place.1 = (f32[320,1024]{1,0:T(8,128)}, f32[4,1024]{1,0:T(4,128)}) custom-call(s32[1024]{0:T(1024)S(1)} %get-tuple-element.11.refs_0_, s32[1024]{0:T(1024)S(1)} %get-tuple-element.10.refs_1_, s32[1,1024]{1,0:T(1,128)S(1)} %bitcast.12, f32[1,1024]{1,0:T(1,128)S(1)} %bitcast.14, f32[2,1024]{1,0:T(2,128)S(1)} %copy-done.4, f32[5120,128]{1,0:T(8,128)S(1)} %bitcast.10), custom_call_target="tpu_custom_call" | custom-call | tf_op jit(solution)/shard_map/place/pallas_call | solution.py:361
  (2 shorter events, 0.0 us)
Async XLA Ops:
  0.6 14.3 %copy-start.1 = (f32[4,256,512]{2,1,0:T(8,128)S(1)}, f32[4,256,512]{2,1,0:T(8,128)}, u32[]{:S(2)}) copy-start(f32[4,256,512]{2,1,0:T(8,128)} %refs_1_.1) | copy-start | bytes 6291460
  0.6 14.3 %copy-start.2 = (s32[4,512]{1,0:T(4,128)S(1)}, s32[4,512]{1,0:T(4,128)}, u32[]{:S(2)}) copy-start(s32[4,512]{1,0:T(4,128)} %refs_0_.1) | copy-start | bytes 24580
  0.7 14.3 %copy-start.3 = (s32[128,16]{0,1:T(8,128)S(1)}, s32[128,16]{0,1:T(8,128)}, u32[]{:S(2)}) copy-start(s32[128,16]{0,1:T(8,128)} %param.12) | copy-start | bytes 24580
  3.4 33.7 %all-to-all-start = ((f32[128,5,4,128]{3,2,1,0:T(4,128)}), f32[128,5,4,128]{3,2,1,0:T(4,128)S(1)}, u32[]{:S(2)}, u32[]{:S(2)}) async-start(f32[128,5,4,128]{3,2,1,0:T(4,128)} %bitcast.5), calls=%async_computation | async-start | bytes 2621440 | tf_op jit(solution)/shard_map/all_to_all | solution.py:287
  20.4 1.9 %copy-start = (bf16[2,1024,1024]{2,1,0:T(8,128)(2,1)}, bf16[2,1024,1024]{2,1,0:T(8,128)(2,1)S(1)}, u32[]{:S(2)}) copy-start(bf16[2,1024,1024]{2,1,0:T(8,128)(2,1)S(1)} %get-tuple-element.7.refs_1_) | copy-start | bytes 12582916
  45.4 4.4 %copy-start.6 = (s32[1024]{0:T(1024)S(1)}, s32[1024]{0:T(1024)}, u32[]{:S(2)}) copy-start(s32[1024]{0:T(1024)} %param.13) | copy-start | bytes 12292
  45.4 40.5 %copy-start.4 = (f32[2,1024]{1,0:T(2,128)S(1)}, f32[2,1024]{1,0:T(2,128)}, u32[]{:S(2)}) copy-start(f32[2,1024]{1,0:T(2,128)} %refs_4_.1) | copy-start | bytes 24580
  45.4 40.5 %copy-start.5 = (f32[1024]{0:T(1024)S(1)}, f32[1024]{0:T(1024)}, u32[]{:S(2)}) copy-start(f32[1024]{0:T(1024)} %param.14) | copy-start | bytes 12292
  45.4 40.5 %all-to-all-start.1 = ((f32[128,10,4,128]{3,2,1,0:T(4,128)}), f32[128,10,4,128]{3,2,1,0:T(4,128)S(1)}, u32[]{:S(2)}, u32[]{:S(2)}) async-start(f32[128,10,4,128]{3,2,1,0:T(4,128)} %bitcast.7), calls=%async_computation.1 | async-start | bytes 5242880 | tf_op jit(solution)/shard_map/all_to_all | solution.py:287

commit v3 on v2

--- a/solution.py
+++ b/solution.py
@@ -81,22 +81,42 @@
         copy.wait()
 
 
-def spread_kernel(slots, src_ref, weights_ref, send_ref, spread_ref, place_ref):
+def spread_kernel(slots, src_ref, weights_ref, send_ref, spread_ref, table_ref, hot_ref):
     blocks, block_rows, block_cols = weights_ref.shape
-    total = spread_ref.shape[2]
+    _, coupled, kept = spread_ref.shape
+    total = hot_ref.shape[1]
     senders = total // slots
+    counts = jnp.zeros((SUB, total), F32)
     for b in range(blocks):
-        slot = src_ref[b : b + 1, :]
-        column = (slot % slots) * senders + slot // slots
-        hot = one_hot(iota((total, block_cols), 0) == column)
+        hot_ref[b] = one_hot(iota((total, block_cols), 0) == src_ref[b : b + 1, :])
+        counts += dot(jnp.ones((SUB, block_cols), BF16), hot_ref[b], ((1,), (1,)))
+    used = counts > 0
+    earlier = one_hot(iota((total, total), 0) < iota((total, total), 1))
+    rank = dot(one_hot(used), earlier, ((1,), (0,))).astype(I32)
+    first_row = iota((SUB, total), 0) == 0
+    digits = jnp.where(first_row, rank // 16, rank % 16).astype(BF16)
+    for b in range(blocks):
+        digit = dot(digits, hot_ref[b], ((1,), (0,))).astype(I32)
+        column = digit[0:1] * 16 + digit[1:2]
+        hot = one_hot(iota((kept, block_cols), 0) == column)
         high, low = split(weights_ref[b])
         summed = dot(high, hot, ((1,), (1,))) + dot(low, hot, ((1,), (1,)))
         high, low = split(summed)
         spread_ref[0, pl.ds(b * block_rows, block_rows), :] = high
         spread_ref[1, pl.ds(b * block_rows, block_rows), :] = low
 
+    slot = iota((SUB, total), 1)
+    digits = jnp.where(first_row, slot // slots, slot % slots).astype(BF16)
+    listed = jnp.where(used[:1], rank[:1], -1)
+    kept_hot = one_hot(iota((kept, total), 0) == listed)
+    digit = dot(digits, kept_hot, ((1,), (1,))).astype(I32)
+    sender, k = digit[0:1], digit[1:2]
+    half = slots // 2
+    table_ref[2:4, :] = jnp.zeros((2, coupled), I32)
+    table_ref[2:3, :kept] = sender * (slots * 5 // 2) + k
+    table_ref[3:4, :kept] = (k // half) * (half * senders) + (k % half) * senders + sender
+
     slots2, oceans = send_ref.shape
-    coupled = blocks * block_rows
     send = send_ref[...]
     ocean, position = jnp.zeros((SUB, coupled), F32), jnp.zeros((SUB, coupled), F32)
     for k in range(slots2):
@@ -107,17 +127,18 @@
     ocean = jnp.where(real, ocean[:1].astype(I32), 0)
     position = jnp.where(real, position[:1].astype(I32), 0)
     half = slots2 // 2
-    place_ref[0:1, :] = ocean * (slots2 * 5 // 2) + position
-    place_ref[1:2, :] = (position // half) * (oceans * half) + ocean * half + position % half
+    table_ref[0:1, :] = ocean * (2 * slots2) + position
+    table_ref[1:2, :] = (position // half) * (oceans * half) + ocean * half + position % half
 
 
 def couple_kernel(
-    slots, slots2, place_any, spread_hbm, recv_ref, out_hbm,
-    place_ref, spread_ref, head_high_ref, head_low_ref, out_ref, tail_ref, block_ref, place_sem, spread_sems, out_sems,
+    slots, slots2, table_any, spread_hbm, recv_ref, out_hbm,
+    table_ref, spread_ref, double_ref, rows_ref, rows_high_ref, rows_low_ref,
+    head_ref, tail_ref, end_ref, block_ref, end_block_ref, table_sem, spread_sems, head_sems, tail_sems,
 ):
-    place_copy = pltpu.make_async_copy(place_any, place_ref, place_sem)
-    place_copy.start()
-    _, coupled, total = spread_ref.shape
+    table_copy = pltpu.make_async_copy(table_any, table_ref, table_sem)
+    table_copy.start()
+    _, coupled, kept = spread_ref.shape
     blocks = block_ref.shape[0]
     each = coupled // blocks
     spread_copies = []
@@ -127,86 +148,122 @@
             pltpu.make_async_copy(spread_hbm.at[:, rows], spread_ref.at[:, rows], spread_sems.at[i])
         )
         spread_copies[-1].start()
-    senders = total // slots
     stride = slots * 5 // 2
+    senders = recv_ref.shape[0] // stride
     left = iota((senders, LANES), 1) < HALF
-    for k in range(slots):
-        rows = pl.ds(k * senders, senders)
-        first = recv_ref[pl.ds(k, senders, stride=stride), :]
-        second = recv_ref[pl.ds(slots + k, senders, stride=stride), :]
-        both = recv_ref[pl.ds(2 * slots + k % (slots // 2), senders, stride=stride), :]
+    for k in range(slots // 2):
+        both = recv_ref[pl.ds(2 * slots + k, senders, stride=stride), :]
         turned = pltpu.roll(both, HALF, 1)
-        third = jnp.where(left, both, turned) if k < slots // 2 else jnp.where(left, turned, both)
-        for i, part in enumerate((first, second, third)):
-            high, low = split(part)
-            head_high_ref[rows, i * LANES : (i + 1) * LANES] = high
-            head_low_ref[rows, i * LANES : (i + 1) * LANES] = low
-    place_copy.wait()
-
-    wide = slots2 * 5 // 2
-    half = slots2 // 2
-    oceans = out_ref.shape[0] // wide
+        double_ref[pl.ds(k * senders, senders), :] = jnp.where(left, both, turned)
+        double_ref[pl.ds((slots // 2 + k) * senders, senders), :] = jnp.where(left, turned, both)
+    table_copy.wait()
+
+    group = 8
+
+    def collect(step, carry):
+        base = pl.multiple_of(step * 4 * group, 4 * group)
+        for more in range(0, 4 * group, group):
+            heads = [table_ref[2, base + more + j] for j in range(group)]
+            tails = [table_ref[3, base + more + j] for j in range(group)]
+            values = [
+                (recv_ref[pl.ds(h, 1), :], recv_ref[pl.ds(h + slots, 1), :], double_ref[pl.ds(t, 1), :])
+                for h, t in zip(heads, tails)
+            ]
+            for j, value in enumerate(values):
+                for c in range(3):
+                    rows_ref[c, pl.ds(base + more + j, 1), :] = value[c]
+        return carry
+
+    lax.fori_loop(0, kept // (4 * group), collect, 0)
+    for c in range(3):
+        lanes = slice(c * LANES, (c + 1) * LANES)
+        rows_high_ref[:, lanes], rows_low_ref[:, lanes] = split(rows_ref[c])
+
     contract = ((1,), (0,))
 
-    def product(i):
-        spread_copies[i].wait()
+    def product(i, lanes):
         rows = pl.ds(i * each, each)
         high, low = spread_ref[0, rows], spread_ref[1, rows]
-        block_ref[i] = (
-            dot(high, head_high_ref[...], contract)
-            + dot(high, head_low_ref[...], contract)
-            + dot(low, head_high_ref[...], contract)
+        return (
+            dot(high, rows_high_ref[:, lanes], contract)
+            + dot(high, rows_low_ref[:, lanes], contract)
+            + dot(low, rows_high_ref[:, lanes], contract)
         )
 
-    def fill(zero):
-        first = jnp.broadcast_to(zero[:, :LANES], (slots2, LANES))
-        second = jnp.broadcast_to(zero[:, LANES : 2 * LANES], (slots2, LANES))
-        third = jnp.broadcast_to(zero[:, 2 * LANES :], (slots2, LANES))
+    oceans = head_ref.shape[0] // (2 * slots2)
+
+    def fill(ref, zero, rows):
+        value = jnp.broadcast_to(zero, (rows, LANES))
 
         def step(o, carry):
-            base = pl.multiple_of(o * wide, SUB)
-            out_ref[pl.ds(base, slots2), :] = first
-            out_ref[pl.ds(base + slots2, slots2), :] = second
-            tail_ref[pl.ds(pl.multiple_of(o * slots2, slots2), slots2), :] = third
+            ref[pl.ds(pl.multiple_of(o * rows, rows), rows), :] = value
             return carry
 
+        lax.fori_loop(0, ref.shape[0] // rows, step, 0, unroll=8)
+
+    def fill_pair(first, second):
+        first = jnp.broadcast_to(first, (slots2, LANES))
+        second = jnp.broadcast_to(second, (slots2, LANES))
+
+        def step(o, carry):
+            base = pl.multiple_of(o * 2 * slots2, 2 * slots2)
+            head_ref[pl.ds(base, slots2), :] = first
+            head_ref[pl.ds(base + slots2, slots2), :] = second
+            return carry
+
         lax.fori_loop(0, oceans, step, 0, unroll=8)
 
     def scatter(i):
-        group = 8
         for base in range(0, each, group):
             rows = range(base, base + group)
-            heads = [place_ref[0, i * each + j] for j in rows]
-            tails = [place_ref[1, i * each + j] for j in rows]
-            values = [[block_ref[i, j : j + 1, c * LANES : (c + 1) * LANES] for c in range(3)] for j in rows]
-            for head, tail, value in zip(heads, tails, values):
-                out_ref[pl.ds(head, 1), :] = value[0]
-                out_ref[pl.ds(head + slots2, 1), :] = value[1]
-                tail_ref[pl.ds(tail, 1), :] = value[2]
-
-    product(0)
-    fill(block_ref[0, 0:1, :])
-    for i in range(1, blocks):
-        product(i)
-        scatter(i - 1)
-    scatter(blocks - 1)
-
-    pieces = out_sems.shape[0]
+            heads = [table_ref[0, i * each + j] for j in rows]
+            values = [(block_ref[i, j : j + 1, :LANES], block_ref[i, j : j + 1, LANES:]) for j in rows]
+            for head, value in zip(heads, values):
+                head_ref[pl.ds(head, 1), :] = value[0]
+                head_ref[pl.ds(head + slots2, 1), :] = value[1]
+
+    def scatter_end(i):
+        for base in range(0, each, group):
+            rows = range(base, base + group)
+            tails = [table_ref[1, i * each + j] for j in rows]
+            values = [end_block_ref[i, j : j + 1, :] for j in rows]
+            for tail, value in zip(tails, values):
+                end_ref[pl.ds(tail, 1), :] = value
+
+    head_lanes, tail_lanes = slice(0, 2 * LANES), slice(2 * LANES, 3 * LANES)
+    for i in range(blocks):
+        spread_copies[i].wait()
+        block_ref[i] = product(i, head_lanes)
+        if i == 0:
+            fill_pair(block_ref[0, 0:1, :LANES], block_ref[0, 0:1, LANES:])
+        scatter(i)
+    pieces = head_sems.shape[0]
     some = oceans // pieces
-    left = iota((half, LANES), 1) < HALF
     copies = []
+    head_view = head_ref.reshape(oceans, 2 * slots2, LANES)
+    out_view = out_hbm.reshape(oceans, slots2 * 5 // 2, LANES)
     for q in range(pieces):
-
-        def merge(step, carry):
-            o = q * some + step
-            near = tail_ref[pl.ds(pl.multiple_of(o * half, half), half), :]
-            far = tail_ref[pl.ds(pl.multiple_of(oceans * half + o * half, half), half), :]
-            out_ref[pl.ds(pl.multiple_of(o * wide + 2 * slots2, SUB), half), :] = jnp.where(left, near, far)
-            return carry
-
-        lax.fori_loop(0, some, merge, 0, unroll=8)
-        part = pl.ds(q * some * wide, some * wide)
-        copies.append(pltpu.make_async_copy(out_ref.at[part], out_hbm.at[part], out_sems.at[q]))
+        part = pl.ds(q * some, some)
+        copies.append(
+            pltpu.make_async_copy(head_view.at[part], out_view.at[part, : 2 * slots2], head_sems.at[q])
+        )
+        copies[-1].start()
+    for i in range(blocks):
+        end_block_ref[i] = product(i, tail_lanes)
+        if i == 0:
+            fill(end_ref, end_block_ref[0, 0:1, :], 16)
+        scatter_end(i)
+    half = slots2 // 2
+    left = iota((some * half, LANES), 1) < HALF
+    tail_view = tail_ref.reshape(oceans, half, LANES)
+    for q in range(pieces):
+        rows = pl.ds(q * some * half, some * half)
+        far = pl.ds((oceans + q * some) * half, some * half)
+        tail_ref[rows] = jnp.where(left, end_ref[rows], end_ref[far])
+        part = pl.ds(q * some, some)
+        copies.append(
+            pltpu.make_async_copy(tail_view.at[part], out_view.at[part, 2 * slots2 :], tail_sems.at[q])
+        )
         copies[-1].start()
     for copy in copies:
         copy.wait()
@@ -282,8 +339,7 @@
 
 
 def exchange(flat, devices):
-    rows = flat.shape[0] // devices
-    shaped = flat.reshape(devices, rows // 4, 4, LANES)
+    shaped = flat.reshape(devices, flat.shape[0] // devices // 4, 4, LANES)
     moved = lax.all_to_all(shaped, "comp", split_axis=0, concat_axis=0, tiled=True)
     return moved.reshape(flat.shape)
 
@@ -318,14 +374,16 @@
     )(in_hbm(send_src.T), in_hbm(src_fields.T))
     received = exchange(outgoing, devices)
 
-    spread, place = pl.pallas_call(
+    kept = 2 * rows
+    spread, table = pl.pallas_call(
         lambda *refs: spread_kernel(slots, *refs),
         out_shape=[
-            jax.ShapeDtypeStruct((2, coupled, total), BF16),
-            jax.ShapeDtypeStruct((2, coupled), I32),
+            jax.ShapeDtypeStruct((2, coupled, kept), BF16),
+            jax.ShapeDtypeStruct((4, coupled), I32),
         ],
         in_specs=[vmem(), vmem(), vmem()],
         out_specs=[vmem(), vmem()],
+        scratch_shapes=[pltpu.VMEM((blocks, total, block_cols), BF16)],
         compiler_params=params(24),
         name="spread_weights",
     )(block_src, weights, coupler_send.T)
@@ -336,20 +394,25 @@
         in_specs=[vmem(), hbm(), vmem()],
         out_specs=hbm(),
         scratch_shapes=[
-            pltpu.SMEM((2, coupled), I32),
-            pltpu.VMEM((2, coupled, total), BF16),
-            pltpu.VMEM((total, 3 * LANES), BF16),
-            pltpu.VMEM((total, 3 * LANES), BF16),
-            pltpu.VMEM((devices * wide, LANES), F32),
+            pltpu.SMEM((4, coupled), I32),
+            pltpu.VMEM((2, coupled, kept), BF16),
+            pltpu.VMEM((devices * slots, LANES), F32),
+            pltpu.VMEM((3, kept, LANES), F32),
+            pltpu.VMEM((kept, 3 * LANES), BF16),
+            pltpu.VMEM((kept, 3 * LANES), BF16),
+            pltpu.VMEM((devices * 2 * slots2, LANES), F32),
+            pltpu.VMEM((devices * slots2 // 2, LANES), F32),
             pltpu.VMEM((devices * slots2, LANES), F32),
-            pltpu.VMEM((4, coupled // 4, 3 * LANES), F32),
+            pltpu.VMEM((4, coupled // 4, 2 * LANES), F32),
+            pltpu.VMEM((4, coupled // 4, LANES), F32),
             dma(()),
             dma((4,)),
-            dma((8,)),
+            dma((4,)),
+            dma((4,)),
         ],
-        compiler_params=params(24),
+        compiler_params=params(51),
         name="couple",
-    )(place, in_hbm(spread), received)
+    )(table, in_hbm(spread), received)
     arrived = exchange(leaving, devices)
 
     base = (ocean_from // slots2) * wide

time: 89.6 us -> 89.4 us (level)
  Pallas kernels: 19.9 us -> 20.8 us
    pallas_call x1, Pallas kernels: 5.39 us -> 6.54 us  [shards(): pl.pallas_call(lambda *refs: spread_kernel(slots, *refs), out_shape=[jax....]
  transfers between devices with their start and end apart: 2 -> 2, of which waited for: 2 -> 2; matrix products, arithmetic and copies ran while one was open for 0% -> 0% of each run, Pallas kernels for 6% -> 7%
where the time goes in v3:
time: 89.4 us; the launch traced here: 89.1 us
  waiting for transfers between devices  50.3 us (56%)
  Pallas kernels  20.8 us (23%)
  starting transfers between devices  15.8 us (18%)
  local copies, waits for them, and re-layouts  1.36 us (2%)
    all_to_all x2, waiting for transfers between devices, exchange(): lax.all_to_all(shaped, 'comp', split_axis=0, concat_axis=0, tiled=True)  50.3 us
    all_to_all x2, starting transfers between devices, exchange(): lax.all_to_all(shaped, 'comp', split_axis=0, concat_axis=0, tiled=True)  15.8 us
    pallas_call x1, Pallas kernels, shards(): pl.pallas_call(lambda *refs: couple_kernel(slots, slots2, *refs), out_sha...  8.09 us
    pallas_call x1, Pallas kernels, shards(): pl.pallas_call(lambda *refs: spread_kernel(slots, *refs), out_shape=[jax....  6.54 us
    pallas_call x1, Pallas kernels, shards(): pl.pallas_call(lambda *refs: place_kernel(slots2, *refs), out_shape=[jax....  3.42 us
    pallas_call x1, Pallas kernels, shards(): pl.pallas_call(gather_kernel, out_shape=jax.ShapeDtypeStruct((devices * n...  2.76 us
  transfers between devices with their start and end apart: 2, of which 2 were waited for; matrix products, arithmetic and copies ran while one was open for 0% of the time, Pallas kernels for 7%

profile of v3, /device:TPU:1, one launch (start us, length us, event | category | flops | bytes accessed | tf_op | source)
XLA Modules:
  0.0 89.1 jit_solution(14380533853199332559)
XLA Ops:
  0.6 0.0 copy-start.1
  0.6 0.0 copy-start.2
  0.7 0.0 copy-start.3
  0.7 2.8 %gather_rows.1 = f32[2560,128]{1,0:T(8,128)} custom-call(s32[8,128]{1,0:T(8,128)} %bitcast.17, f32[320,256]{1,0:T(8,128)} %bitcast.16), custom_call_target="tpu_custom_call" | custom-call | tf_op jit(solution)/shard_map/gather_rows/pallas_call | solution.py:360
  3.4 11.5 %all-to-all-start = ((f32[128,5,4,128]{3,2,1,0:T(4,128)}), f32[128,5,4,128]{3,2,1,0:T(4,128)S(1)}, u32[]{:S(2)}, u32[]{:S(2)}) async-start(f32[128,5,4,128]{3,2,1,0:T(4,128)} %bitcast.5), calls=%async_computation | async-start | bytes 2621440 | tf_op jit(solution)/shard_map/all_to_all | solution.py:343
  14.9 0.0 copy-done.1
  15.0 0.0 copy-done.2
  15.0 0.0 copy-done.3
  15.0 6.5 %spread_weights.1 = (bf16[2,1024,512]{2,1,0:T(8,128)(2,1)S(1)}, s32[4,1024]{1,0:T(4,128)S(1)}) custom-call(s32[4,512]{1,0:T(4,128)S(1)} %copy-done.2, f32[4,256,512]{2,1,0:T(8,128)S(1)} %copy-done.1, s32[16,128]{1,0:T(8,128)S(1)} %bitcast.13), custom_call_target="tpu_custom_call" | custom-call | tf_op jit(solution)/shard_map/spread_weights/pallas_call | solution.py:378
  21.5 0.0 copy-start
  21.5 1.3 %copy-done = bf16[2,1024,512]{2,1,0:T(8,128)(2,1)} copy-done((bf16[2,1024,512]{2,1,0:T(8,128)(2,1)}, bf16[2,1024,512]{2,1,0:T(8,128)(2,1)S(1)}, u32[]{:S(2)}) %copy-start) | copy-done | bytes 2097176
  22.9 14.2 %all-to-all-done = f32[128,5,4,128]{3,2,1,0:T(4,128)S(1)} async-done(((f32[128,5,4,128]{3,2,1,0:T(4,128)}), f32[128,5,4,128]{3,2,1,0:T(4,128)S(1)}, u32[]{:S(2)}, u32[]{:S(2)}) %all-to-all-start) | async-done | bytes 1310752 | tf_op jit(solution)/shard_map/all_to_all | solution.py:343
  37.1 8.1 %couple.1 = f32[5120,128]{1,0:T(8,128)} custom-call(s32[4,1024]{1,0:T(4,128)S(1)} %get-tuple-element.6.refs_0_, bf16[2,1024,512]{2,1,0:T(8,128)(2,1)} %copy-done, f32[2560,128]{1,0:T(8,128)S(1)} %bitcast.11), custom_call_target="tpu_custom_call" | custom-call | tf_op jit(solution)/shard_map/couple/pallas_call | solution.py:391
  45.2 0.0 copy-start.6
  45.2 0.0 copy-start.4
  45.2 0.0 copy-start.5
  45.2 4.3 %all-to-all-start.1 = ((f32[128,10,4,128]{3,2,1,0:T(4,128)}), f32[128,10,4,128]{3,2,1,0:T(4,128)S(1)}, u32[]{:S(2)}, u32[]{:S(2)}) async-start(f32[128,10,4,128]{3,2,1,0:T(4,128)} %bitcast.15), calls=%async_computation.1 | async-start | bytes 5242880 | tf_op jit(solution)/shard_map/all_to_all | solution.py:343
  49.6 0.0 copy-done.6
  49.6 36.1 %all-to-all-done.1 = f32[128,10,4,128]{3,2,1,0:T(4,128)S(1)} async-done(((f32[128,10,4,128]{3,2,1,0:T(4,128)}), f32[128,10,4,128]{3,2,1,0:T(4,128)S(1)}, u32[]{:S(2)}, u32[]{:S(2)}) %all-to-all-start.1) | async-done | bytes 2621472 | tf_op jit(solution)/shard_map/all_to_all | solution.py:343
  85.7 0.0 copy-done.4
  85.7 0.0 copy-done.5
  85.7 3.4 %place.1 = (f32[320,1024]{1,0:T(8,128)}, f32[4,1024]{1,0:T(4,128)}) custom-call(s32[1024]{0:T(1024)S(1)} %get-tuple-element.11.refs_0_, s32[1024]{0:T(1024)S(1)} %get-tuple-element.10.refs_1_, s32[1,1024]{1,0:T(1,128)S(1)} %bitcast.12, f32[1,1024]{1,0:T(1,128)S(1)} %bitcast.14, f32[2,1024]{1,0:T(2,128)S(1)} %copy-done.4, f32[5120,128]{1,0:T(8,128)S(1)} %bitcast.10), custom_call_target="tpu_custom_call" | custom-call | tf_op jit(solution)/shard_map/place/pallas_call | solution.py:424
  (2 shorter events, 0.0 us)
Async XLA Ops:
  0.6 14.3 %copy-start.1 = (f32[4,256,512]{2,1,0:T(8,128)S(1)}, f32[4,256,512]{2,1,0:T(8,128)}, u32[]{:S(2)}) copy-start(f32[4,256,512]{2,1,0:T(8,128)} %refs_1_.1) | copy-start | bytes 6291460
  0.6 14.3 %copy-start.2 = (s32[4,512]{1,0:T(4,128)S(1)}, s32[4,512]{1,0:T(4,128)}, u32[]{:S(2)}) copy-start(s32[4,512]{1,0:T(4,128)} %refs_0_.1) | copy-start | bytes 24580
  0.7 14.3 %copy-start.3 = (s32[128,16]{0,1:T(8,128)S(1)}, s32[128,16]{0,1:T(8,128)}, u32[]{:S(2)}) copy-start(s32[128,16]{0,1:T(8,128)} %param.12) | copy-start | bytes 24580
  3.4 33.7 %all-to-all-start = ((f32[128,5,4,128]{3,2,1,0:T(4,128)}), f32[128,5,4,128]{3,2,1,0:T(4,128)S(1)}, u32[]{:S(2)}, u32[]{:S(2)}) async-start(f32[128,5,4,128]{3,2,1,0:T(4,128)} %bitcast.5), calls=%async_computation | async-start | bytes 2621440 | tf_op jit(solution)/shard_map/all_to_all | solution.py:343
  21.5 1.3 %copy-start = (bf16[2,1024,512]{2,1,0:T(8,128)(2,1)}, bf16[2,1024,512]{2,1,0:T(8,128)(2,1)S(1)}, u32[]{:S(2)}) copy-start(bf16[2,1024,512]{2,1,0:T(8,128)(2,1)S(1)} %get-tuple-element.7.refs_1_) | copy-start | bytes 6291460
  45.2 4.4 %copy-start.6 = (s32[1024]{0:T(1024)S(1)}, s32[1024]{0:T(1024)}, u32[]{:S(2)}) copy-start(s32[1024]{0:T(1024)} %param.13) | copy-start | bytes 12292
  45.2 40.5 %copy-start.4 = (f32[2,1024]{1,0:T(2,128)S(1)}, f32[2,1024]{1,0:T(2,128)}, u32[]{:S(2)}) copy-start(f32[2,1024]{1,0:T(2,128)} %refs_4_.1) | copy-start | bytes 24580
  45.2 40.5 %copy-start.5 = (f32[1024]{0:T(1024)S(1)}, f32[1024]{0:T(1024)}, u32[]{:S(2)}) copy-start(f32[1024]{0:T(1024)} %param.14) | copy-start | bytes 12292
  45.2 40.5 %all-to-all-start.1 = ((f32[128,10,4,128]{3,2,1,0:T(4,128)}), f32[128,10,4,128]{3,2,1,0:T(4,128)S(1)}, u32[]{:S(2)}, u32[]{:S(2)}) async-start(f32[128,10,4,128]{3,2,1,0:T(4,128)} %bitcast.15), calls=%async_computation.1 | async-start | bytes 5242880 | tf_op jit(solution)/shard_map/all_to_all | solution.py:343

commit v4 on v3

--- a/solution.py
+++ b/solution.py
@@ -81,9 +81,9 @@
         copy.wait()
 
 
-def spread_kernel(slots, src_ref, weights_ref, send_ref, spread_ref, table_ref, hot_ref):
+def spread_kernel(slots, src_ref, weights_ref, send_ref, spread_ref, take_ref, table_ref, hot_ref):
     blocks, block_rows, block_cols = weights_ref.shape
-    _, coupled, kept = spread_ref.shape
+    coupled, kept = spread_ref.shape[0], spread_ref.shape[1] // 2
     total = hot_ref.shape[1]
     senders = total // slots
     counts = jnp.zeros((SUB, total), F32)
@@ -102,8 +102,8 @@
         high, low = split(weights_ref[b])
         summed = dot(high, hot, ((1,), (1,))) + dot(low, hot, ((1,), (1,)))
         high, low = split(summed)
-        spread_ref[0, pl.ds(b * block_rows, block_rows), :] = high
-        spread_ref[1, pl.ds(b * block_rows, block_rows), :] = low
+        spread_ref[pl.ds(b * block_rows, block_rows), :kept] = high
+        spread_ref[pl.ds(b * block_rows, block_rows), kept:] = low
 
     slot = iota((SUB, total), 1)
     digits = jnp.where(first_row, slot // slots, slot % slots).astype(BF16)
@@ -112,9 +112,8 @@
     digit = dot(digits, kept_hot, ((1,), (1,))).astype(I32)
     sender, k = digit[0:1], digit[1:2]
     half = slots // 2
-    table_ref[2:4, :] = jnp.zeros((2, coupled), I32)
-    table_ref[2:3, :kept] = sender * (slots * 5 // 2) + k
-    table_ref[3:4, :kept] = (k // half) * (half * senders) + (k % half) * senders + sender
+    take_ref[0:1, :] = sender * (slots * 5 // 2) + k
+    take_ref[1:2, :] = (k // half) * (half * senders) + (k % half) * senders + sender
 
     slots2, oceans = send_ref.shape
     send = send_ref[...]
@@ -132,20 +131,22 @@
 
 
 def couple_kernel(
-    slots, slots2, table_any, spread_hbm, recv_ref, out_hbm,
-    table_ref, spread_ref, double_ref, rows_ref, rows_high_ref, rows_low_ref,
-    head_ref, tail_ref, end_ref, block_ref, end_block_ref, table_sem, spread_sems, head_sems, tail_sems,
+    slots, slots2, take_any, table_any, spread_hbm, recv_ref, out_hbm,
+    take_ref, table_ref, spread_ref, double_ref, rows_ref, rows_high_ref, rows_low_ref,
+    head_ref, tail_ref, end_ref, block_ref, end_block_ref, table_sems, spread_sems, head_sems, tail_sems,
 ):
-    table_copy = pltpu.make_async_copy(table_any, table_ref, table_sem)
+    coupled, kept = spread_ref.shape[0], spread_ref.shape[1] // 2
+    take_copy = pltpu.make_async_copy(take_any, take_ref, table_sems.at[0])
+    take_copy.start()
+    table_copy = pltpu.make_async_copy(table_any, table_ref, table_sems.at[1])
     table_copy.start()
-    _, coupled, kept = spread_ref.shape
     blocks = block_ref.shape[0]
     each = coupled // blocks
     spread_copies = []
     for i in range(blocks):
         rows = pl.ds(i * each, each)
         spread_copies.append(
-            pltpu.make_async_copy(spread_hbm.at[:, rows], spread_ref.at[:, rows], spread_sems.at[i])
+            pltpu.make_async_copy(spread_hbm.at[rows], spread_ref.at[rows], spread_sems.at[i])
         )
         spread_copies[-1].start()
     stride = slots * 5 // 2
@@ -156,62 +157,37 @@
         turned = pltpu.roll(both, HALF, 1)
         double_ref[pl.ds(k * senders, senders), :] = jnp.where(left, both, turned)
         double_ref[pl.ds((slots // 2 + k) * senders, senders), :] = jnp.where(left, turned, both)
-    table_copy.wait()
+    take_copy.wait()
 
     group = 8
 
-    def collect(step, carry):
-        base = pl.multiple_of(step * 4 * group, 4 * group)
-        for more in range(0, 4 * group, group):
-            heads = [table_ref[2, base + more + j] for j in range(group)]
-            tails = [table_ref[3, base + more + j] for j in range(group)]
-            values = [
-                (recv_ref[pl.ds(h, 1), :], recv_ref[pl.ds(h + slots, 1), :], double_ref[pl.ds(t, 1), :])
-                for h, t in zip(heads, tails)
-            ]
-            for j, value in enumerate(values):
-                for c in range(3):
-                    rows_ref[c, pl.ds(base + more + j, 1), :] = value[c]
-        return carry
-
-    lax.fori_loop(0, kept // (4 * group), collect, 0)
+    for base in range(0, kept, group):
+        rows = range(base, base + group)
+        heads = [take_ref[0, j] for j in rows]
+        tails = [take_ref[1, j] for j in rows]
+        values = [
+            (recv_ref[pl.ds(h, 1), :], recv_ref[pl.ds(h + slots, 1), :], double_ref[pl.ds(t, 1), :])
+            for h, t in zip(heads, tails)
+        ]
+        for j, value in zip(rows, values):
+            for c in range(3):
+                rows_ref[c, j : j + 1, :] = value[c]
     for c in range(3):
         lanes = slice(c * LANES, (c + 1) * LANES)
-        rows_high_ref[:, lanes], rows_low_ref[:, lanes] = split(rows_ref[c])
+        high, low = split(rows_ref[c])
+        rows_high_ref[:kept, lanes] = high
+        rows_high_ref[kept:, lanes] = high
+        rows_low_ref[:, lanes] = low
 
     contract = ((1,), (0,))
 
     def product(i, lanes):
         rows = pl.ds(i * each, each)
-        high, low = spread_ref[0, rows], spread_ref[1, rows]
-        return (
-            dot(high, rows_high_ref[:, lanes], contract)
-            + dot(high, rows_low_ref[:, lanes], contract)
-            + dot(low, rows_high_ref[:, lanes], contract)
+        return dot(spread_ref[rows], rows_high_ref[:, lanes], contract) + dot(
+            spread_ref[rows, :kept], rows_low_ref[:, lanes], contract
         )
 
     oceans = head_ref.shape[0] // (2 * slots2)
-
-    def fill(ref, zero, rows):
-        value = jnp.broadcast_to(zero, (rows, LANES))
-
-        def step(o, carry):
-            ref[pl.ds(pl.multiple_of(o * rows, rows), rows), :] = value
-            return carry
-
-        lax.fori_loop(0, ref.shape[0] // rows, step, 0, unroll=8)
-
-    def fill_pair(first, second):
-        first = jnp.broadcast_to(first, (slots2, LANES))
-        second = jnp.broadcast_to(second, (slots2, LANES))
-
-        def step(o, carry):
-            base = pl.multiple_of(o * 2 * slots2, 2 * slots2)
-            head_ref[pl.ds(base, slots2), :] = first
-            head_ref[pl.ds(base + slots2, slots2), :] = second
-            return carry
-
-        lax.fori_loop(0, oceans, step, 0, unroll=8)
 
     def scatter(i):
         for base in range(0, each, group):
@@ -231,11 +207,17 @@
                 end_ref[pl.ds(tail, 1), :] = value
 
     head_lanes, tail_lanes = slice(0, 2 * LANES), slice(2 * LANES, 3 * LANES)
+    table_copy.wait()
+    for copy in spread_copies:
+        copy.wait()
     for i in range(blocks):
-        spread_copies[i].wait()
         block_ref[i] = product(i, head_lanes)
-        if i == 0:
-            fill_pair(block_ref[0, 0:1, :LANES], block_ref[0, 0:1, LANES:])
+    first = jnp.broadcast_to(block_ref[0, 0:1, :LANES], (slots2, LANES))
+    second = jnp.broadcast_to(block_ref[0, 0:1, LANES:], (slots2, LANES))
+    for o in range(oceans):
+        head_ref[2 * o * slots2 : (2 * o + 1) * slots2, :] = first
+        head_ref[(2 * o + 1) * slots2 : (2 * o + 2) * slots2, :] = second
+    for i in range(blocks):
         scatter(i)
     pieces = head_sems.shape[0]
     some = oceans // pieces
@@ -250,8 +232,8 @@
         copies[-1].start()
     for i in range(blocks):
         end_block_ref[i] = product(i, tail_lanes)
-        if i == 0:
-            fill(end_ref, end_block_ref[0, 0:1, :], 16)
+    end_ref[...] = jnp.broadcast_to(end_block_ref[0, 0:1, :], end_ref.shape)
+    for i in range(blocks):
         scatter_end(i)
     half = slots2 // 2
     left = iota((some * half, LANES), 1) < HALF
@@ -270,10 +252,10 @@
 
 
 def place_kernel(
-    slots2, head_ref, tail_ref, lower_ref, temp_ref, current_ref, arrived_ref, out_hbm, flux_ref, out_ref, sems,
+    slots2, slot_ref, lower_ref, temp_ref, current_ref, arrived_ref, out_hbm, flux_hbm,
+    out_ref, flux_ref, sems,
 ):
-    blocks = sems.shape[0]
-    columns = out_ref.shape[1]
+    blocks = sems.shape[0] - 1
     row = iota((SUB, LANES), 0)
 
     def pick(slots):
@@ -284,23 +266,18 @@
 
     def block(b):
         base = b * LANES
-        if not isinstance(b, int):
-            base = pl.multiple_of(base, LANES)
         first, second, third = [], [], []
-        for j in range(0, LANES, SUB):
-            heads = [head_ref[base + j + i] for i in range(SUB)]
-            tails = [tail_ref[base + j + i] for i in range(SUB)]
+        for j in range(base, base + LANES, SUB):
+            heads = [slot_ref[0, j + i] for i in range(SUB)]
+            tails = [slot_ref[1, j + i] for i in range(SUB)]
             first.append(pick(heads))
             second.append(pick([h + slots2 for h in heads]))
             third.append(pick(tails))
-        first = jnp.concatenate(first, axis=0).T
-        second = jnp.concatenate(second, axis=0).T
-        third = jnp.concatenate(third, axis=0).T
+        first, second, third = (jnp.concatenate(x, axis=0).T for x in (first, second, third))
         lanes = pl.ds(base, LANES)
         out_ref[b, :LANES, :] = first
         out_ref[b, LANES : 2 * LANES, :] = second
         out_ref[b, 2 * LANES :, :] = jnp.where(lower_ref[:, lanes] > 0, third[:HALF], third[HALF:])
-        pltpu.make_async_copy(out_ref.at[b], out_hbm.at[:, lanes], sems.at[b]).start()
         wind_east = first[0:1]
         wind_north = first[LEV : LEV + 1]
         air_temp = first[2 * LEV : 2 * LEV + 1]
@@ -312,10 +289,20 @@
         flux_ref[2:3, lanes] = scale * (wind_east - current_ref[0:1, lanes])
         flux_ref[3:4, lanes] = scale * (wind_north - current_ref[1:2, lanes])
 
-    for b in range(blocks):
-        block(b)
-    for b in range(blocks):
-        pltpu.make_async_copy(out_ref.at[b], out_hbm.at[:, pl.ds(b * LANES, LANES)], sems.at[b]).wait()
+    copies = []
+    phases = 2
+    for phase in range(phases):
+        some = range(phase * blocks // phases, (phase + 1) * blocks // phases)
+        for b in some:
+            block(b)
+        for b in some:
+            lanes = pl.ds(b * LANES, LANES)
+            copies.append(pltpu.make_async_copy(out_ref.at[b], out_hbm.at[:, lanes], sems.at[b]))
+            copies[-1].start()
+    copies.append(pltpu.make_async_copy(flux_ref, flux_hbm, sems.at[blocks]))
+    copies[-1].start()
+    for copy in copies:
+        copy.wait()
 
 
 def vmem():
@@ -375,14 +362,15 @@
     received = exchange(outgoing, devices)
 
     kept = 2 * rows
-    spread, table = pl.pallas_call(
+    spread, take, table = pl.pallas_call(
         lambda *refs: spread_kernel(slots, *refs),
         out_shape=[
-            jax.ShapeDtypeStruct((2, coupled, kept), BF16),
-            jax.ShapeDtypeStruct((4, coupled), I32),
+            jax.ShapeDtypeStruct((coupled, 2 * kept), BF16),
+            jax.ShapeDtypeStruct((2, kept), I32),
+            jax.ShapeDtypeStruct((2, coupled), I32),
         ],
         in_specs=[vmem(), vmem(), vmem()],
-        out_specs=[vmem(), vmem()],
+        out_specs=[vmem(), vmem(), vmem()],
         scratch_shapes=[pltpu.VMEM((blocks, total, block_cols), BF16)],
         compiler_params=params(24),
         name="spread_weights",
@@ -391,28 +379,29 @@
     leaving = pl.pallas_call(
         lambda *refs: couple_kernel(slots, slots2, *refs),
         out_shape=jax.ShapeDtypeStruct((devices * wide, LANES), F32),
-        in_specs=[vmem(), hbm(), vmem()],
+        in_specs=[vmem(), vmem(), hbm(), vmem()],
         out_specs=hbm(),
         scratch_shapes=[
-            pltpu.SMEM((4, coupled), I32),
-            pltpu.VMEM((2, coupled, kept), BF16),
+            pltpu.SMEM((2, kept), I32),
+            pltpu.SMEM((2, coupled), I32),
+            pltpu.VMEM((coupled, 2 * kept), BF16),
             pltpu.VMEM((devices * slots, LANES), F32),
             pltpu.VMEM((3, kept, LANES), F32),
-            pltpu.VMEM((kept, 3 * LANES), BF16),
+            pltpu.VMEM((2 * kept, 3 * LANES), BF16),
             pltpu.VMEM((kept, 3 * LANES), BF16),
             pltpu.VMEM((devices * 2 * slots2, LANES), F32),
             pltpu.VMEM((devices * slots2 // 2, LANES), F32),
             pltpu.VMEM((devices * slots2, LANES), F32),
-            pltpu.VMEM((4, coupled // 4, 2 * LANES), F32),
-            pltpu.VMEM((4, coupled // 4, LANES), F32),
-            dma(()),
-            dma((4,)),
+            pltpu.VMEM((2, coupled // 2, 2 * LANES), F32),
+            pltpu.VMEM((2, coupled // 2, LANES), F32),
+            dma((2,)),
+            dma((2,)),
             dma((4,)),
             dma((4,)),
         ],
         compiler_params=params(51),
         name="couple",
-    )(table, in_hbm(spread), received)
+    )(take, table, in_hbm(spread), received)
     arrived = exchange(leaving, devices)
 
     base = (ocean_from // slots2) * wide
@@ -424,15 +413,16 @@
     remapped, fluxes = pl.pallas_call(
         lambda *refs: place_kernel(slots2, *refs),
         out_shape=[jax.ShapeDtypeStruct((columns, cells), F32), jax.ShapeDtypeStruct((4, cells), F32)],
-        in_specs=[smem(), smem(), vmem(), vmem(), vmem(), vmem()],
-        out_specs=[hbm(), vmem()],
+        in_specs=[smem(), vmem(), vmem(), vmem(), vmem()],
+        out_specs=[hbm(), hbm()],
         scratch_shapes=[
             pltpu.VMEM((cells // LANES, columns, LANES), F32),
-            dma((cells // LANES,)),
+            pltpu.VMEM((4, cells), F32),
+            dma((cells // LANES + 1,)),
         ],
         compiler_params=params(16),
         name="place",
-    )(head, tail, lower, surface_temp[None], ocean_current, arrived)
+    )(jnp.stack([head, tail]), lower, surface_temp[None], ocean_current, arrived)
     return (remapped.T, fluxes)
 
 

time: 89.4 us -> 86.8 us (0.971)
  Pallas kernels: 20.8 us -> 18.2 us
    pallas_call x1, Pallas kernels: 8.09 us -> 5.92 us  [shards(): pl.pallas_call(lambda *refs: couple_kernel(slots, slots2, *refs), out_sha...]
  transfers between devices with their start and end apart: 2 -> 2, of which waited for: 2 -> 2; matrix products, arithmetic and copies ran while one was open for 0% -> 0% of each run, Pallas kernels for 7% -> 8%
where the time goes in v4:
time: 86.8 us; the launch traced here: 86.5 us
  waiting for transfers between devices  50.3 us (58%)
  Pallas kernels  18.2 us (21%)
  starting transfers between devices  15.8 us (18%)
  local copies, waits for them, and re-layouts  1.36 us (2%)
    all_to_all x2, waiting for transfers between devices, exchange(): lax.all_to_all(shaped, 'comp', split_axis=0, concat_axis=0, tiled=True)  50.3 us
    all_to_all x2, starting transfers between devices, exchange(): lax.all_to_all(shaped, 'comp', split_axis=0, concat_axis=0, tiled=True)  15.8 us
    pallas_call x1, Pallas kernels, shards(): pl.pallas_call(lambda *refs: spread_kernel(slots, *refs), out_shape=[jax....  6.54 us
    pallas_call x1, Pallas kernels, shards(): pl.pallas_call(lambda *refs: couple_kernel(slots, slots2, *refs), out_sha...  5.92 us
    pallas_call x1, Pallas kernels, shards(): pl.pallas_call(lambda *refs: place_kernel(slots2, *refs), out_shape=[jax....  2.98 us
    pallas_call x1, Pallas kernels, shards(): pl.pallas_call(gather_kernel, out_shape=jax.ShapeDtypeStruct((devices * n...  2.76 us
  transfers between devices with their start and end apart: 2, of which 2 were waited for; matrix products, arithmetic and copies ran while one was open for 0% of the time, Pallas kernels for 8%

profile of v4, /device:TPU:1, one launch (start us, length us, event | category | flops | bytes accessed | tf_op | source)
XLA Modules:
  0.0 86.5 jit_solution(4781181624132196507)
XLA Ops:
  0.6 0.0 copy-start.1
  0.6 0.0 copy-start.2
  0.7 0.0 copy-start.3
  0.7 2.8 %gather_rows.1 = f32[2560,128]{1,0:T(8,128)} custom-call(s32[8,128]{1,0:T(8,128)} %bitcast.21, f32[320,256]{1,0:T(8,128)} %bitcast.18), custom_call_target="tpu_custom_call" | custom-call | tf_op jit(solution)/shard_map/gather_rows/pallas_call | solution.py:347
  3.4 11.5 %all-to-all-start = ((f32[128,5,4,128]{3,2,1,0:T(4,128)}), f32[128,5,4,128]{3,2,1,0:T(4,128)S(1)}, u32[]{:S(2)}, u32[]{:S(2)}) async-start(f32[128,5,4,128]{3,2,1,0:T(4,128)} %bitcast.7), calls=%async_computation | async-start | bytes 2621440 | tf_op jit(solution)/shard_map/all_to_all | solution.py:330
  14.9 0.0 copy-done.1
  15.0 0.0 copy-done.2
  15.0 0.0 copy-done.3
  15.0 6.5 %spread_weights.1 = (bf16[1024,1024]{1,0:T(8,128)(2,1)S(1)}, s32[2,512]{1,0:T(2,128)S(1)}, s32[2,1024]{1,0:T(2,128)S(1)}) custom-call(s32[4,512]{1,0:T(4,128)S(1)} %copy-done.2, f32[4,256,512]{2,1,0:T(8,128)S(1)} %copy-done.1, s32[16,128]{1,0:T(8,128)S(1)} %bitcast.15), custom_call_target="tpu_custom_call" | custom-call | tf_op jit(solution)/shard_map/spread_weights/pallas_call | solution.py:365
  21.5 0.0 copy-start
  21.5 1.3 %copy-done = bf16[1024,1024]{1,0:T(8,128)(2,1)} copy-done((bf16[1024,1024]{1,0:T(8,128)(2,1)}, bf16[1024,1024]{1,0:T(8,128)(2,1)S(1)}, u32[]{:S(2)}) %copy-start) | copy-done | bytes 2097176
  22.9 14.2 %all-to-all-done = f32[128,5,4,128]{3,2,1,0:T(4,128)S(1)} async-done(((f32[128,5,4,128]{3,2,1,0:T(4,128)}), f32[128,5,4,128]{3,2,1,0:T(4,128)S(1)}, u32[]{:S(2)}, u32[]{:S(2)}) %all-to-all-start) | async-done | bytes 1310752 | tf_op jit(solution)/shard_map/all_to_all | solution.py:330
  37.1 5.9 %couple.1 = f32[5120,128]{1,0:T(8,128)} custom-call(s32[2,512]{1,0:T(2,128)S(1)} %get-tuple-element.7.refs_0_, s32[2,1024]{1,0:T(2,128)S(1)} %get-tuple-element.8.refs_1_, bf16[1024,1024]{1,0:T(8,128)(2,1)} %copy-done, f32[2560,128]{1,0:T(8,128)S(1)} %bitcast.13), custom_call_target="tpu_custom_call" | custom-call | tf_op jit(solution)/shard_map/couple/pallas_call | solution.py:379
  43.0 0.0 copy-start.6
  43.0 0.0 copy-start.4
  43.0 0.0 copy-start.5
  43.1 4.3 %all-to-all-start.1 = ((f32[128,10,4,128]{3,2,1,0:T(4,128)}), f32[128,10,4,128]{3,2,1,0:T(4,128)S(1)}, u32[]{:S(2)}, u32[]{:S(2)}) async-start(f32[128,10,4,128]{3,2,1,0:T(4,128)} %bitcast.17), calls=%async_computation.1 | async-start | bytes 5242880 | tf_op jit(solution)/shard_map/all_to_all | solution.py:330
  47.4 0.0 copy-done.6
  47.5 36.1 %all-to-all-done.1 = f32[128,10,4,128]{3,2,1,0:T(4,128)S(1)} async-done(((f32[128,10,4,128]{3,2,1,0:T(4,128)}), f32[128,10,4,128]{3,2,1,0:T(4,128)S(1)}, u32[]{:S(2)}, u32[]{:S(2)}) %all-to-all-start.1) | async-done | bytes 2621472 | tf_op jit(solution)/shard_map/all_to_all | solution.py:330
  83.5 0.0 copy-done.4
  83.5 0.0 copy-done.5
  83.5 3.0 %place.1 = (f32[320,1024]{1,0:T(8,128)}, f32[4,1024]{1,0:T(4,128)}) custom-call(s32[2,1024]{1,0:T(2,128)S(1)} %pad_add_fusion.refs_0_, s32[1,1024]{1,0:T(1,128)S(1)} %bitcast.14, f32[1,1024]{1,0:T(1,128)S(1)} %bitcast.16, f32[2,1024]{1,0:T(2,128)S(1)} %copy-done.4, f32[5120,128]{1,0:T(8,128)S(1)} %bitcast.12), custom_call_target="tpu_custom_call" | custom-call | tf_op jit(solution)/shard_map/place/pallas_call | solution.py:413
  (3 shorter events, 0.0 us)
Async XLA Ops:
  0.6 14.3 %copy-start.1 = (f32[4,256,512]{2,1,0:T(8,128)S(1)}, f32[4,256,512]{2,1,0:T(8,128)}, u32[]{:S(2)}) copy-start(f32[4,256,512]{2,1,0:T(8,128)} %refs_1_.1) | copy-start | bytes 6291460
  0.6 14.3 %copy-start.2 = (s32[4,512]{1,0:T(4,128)S(1)}, s32[4,512]{1,0:T(4,128)}, u32[]{:S(2)}) copy-start(s32[4,512]{1,0:T(4,128)} %refs_0_.1) | copy-start | bytes 24580
  0.7 14.3 %copy-start.3 = (s32[128,16]{0,1:T(8,128)S(1)}, s32[128,16]{0,1:T(8,128)}, u32[]{:S(2)}) copy-start(s32[128,16]{0,1:T(8,128)} %param.12) | copy-start | bytes 24580
  3.4 33.7 %all-to-all-start = ((f32[128,5,4,128]{3,2,1,0:T(4,128)}), f32[128,5,4,128]{3,2,1,0:T(4,128)S(1)}, u32[]{:S(2)}, u32[]{:S(2)}) async-start(f32[128,5,4,128]{3,2,1,0:T(4,128)} %bitcast.7), calls=%async_computation | async-start | bytes 2621440 | tf_op jit(solution)/shard_map/all_to_all | solution.py:330
  21.5 1.3 %copy-start = (bf16[1024,1024]{1,0:T(8,128)(2,1)}, bf16[1024,1024]{1,0:T(8,128)(2,1)S(1)}, u32[]{:S(2)}) copy-start(bf16[1024,1024]{1,0:T(8,128)(2,1)S(1)} %get-tuple-element.9.refs_2_) | copy-start | bytes 6291460
  43.0 4.4 %copy-start.6 = (s32[1024]{0:T(1024)S(1)}, s32[1024]{0:T(1024)}, u32[]{:S(2)}) copy-start(s32[1024]{0:T(1024)} %param.13) | copy-start | bytes 12292
  43.0 40.5 %copy-start.4 = (f32[2,1024]{1,0:T(2,128)S(1)}, f32[2,1024]{1,0:T(2,128)}, u32[]{:S(2)}) copy-start(f32[2,1024]{1,0:T(2,128)} %refs_3_.1) | copy-start | bytes 24580
  43.0 40.5 %copy-start.5 = (f32[1024]{0:T(1024)S(1)}, f32[1024]{0:T(1024)}, u32[]{:S(2)}) copy-start(f32[1024]{0:T(1024)} %param.14) | copy-start | bytes 12292
  43.1 40.5 %all-to-all-start.1 = ((f32[128,10,4,128]{3,2,1,0:T(4,128)}), f32[128,10,4,128]{3,2,1,0:T(4,128)S(1)}, u32[]{:S(2)}, u32[]{:S(2)}) async-start(f32[128,10,4,128]{3,2,1,0:T(4,128)} %bitcast.17), calls=%async_computation.1 | async-start | bytes 5242880 | tf_op jit(solution)/shard_map/all_to_all | solution.py:330

commit v5 on v4

--- a/solution.py
+++ b/solution.py
@@ -83,7 +83,7 @@
 
 def spread_kernel(slots, src_ref, weights_ref, send_ref, spread_ref, take_ref, table_ref, hot_ref):
     blocks, block_rows, block_cols = weights_ref.shape
-    coupled, kept = spread_ref.shape[0], spread_ref.shape[1] // 2
+    coupled, kept = spread_ref.shape[0], spread_ref.shape[1] // 3
     total = hot_ref.shape[1]
     senders = total // slots
     counts = jnp.zeros((SUB, total), F32)
@@ -102,8 +102,8 @@
         high, low = split(weights_ref[b])
         summed = dot(high, hot, ((1,), (1,))) + dot(low, hot, ((1,), (1,)))
         high, low = split(summed)
-        spread_ref[pl.ds(b * block_rows, block_rows), :kept] = high
-        spread_ref[pl.ds(b * block_rows, block_rows), kept:] = low
+        for i, part in enumerate((high, low, high)):
+            spread_ref[b * block_rows : (b + 1) * block_rows, i * kept : (i + 1) * kept] = part
 
     slot = iota((SUB, total), 1)
     digits = jnp.where(first_row, slot // slots, slot % slots).astype(BF16)
@@ -131,24 +131,17 @@
 
 
 def couple_kernel(
-    slots, slots2, take_any, table_any, spread_hbm, recv_ref, out_hbm,
-    take_ref, table_ref, spread_ref, double_ref, rows_ref, rows_high_ref, rows_low_ref,
-    head_ref, tail_ref, end_ref, block_ref, end_block_ref, table_sems, spread_sems, head_sems, tail_sems,
+    slots, slots2, take_any, table_any, spread_ref, recv_ref, out_hbm,
+    take_ref, table_ref, double_ref, stacked_ref,
+    head_ref, tail_ref, end_ref, block_ref, end_block_ref, table_sems, head_sems, tail_sems,
 ):
-    coupled, kept = spread_ref.shape[0], spread_ref.shape[1] // 2
+    coupled, kept = spread_ref.shape[0], spread_ref.shape[1] // 3
     take_copy = pltpu.make_async_copy(take_any, take_ref, table_sems.at[0])
     take_copy.start()
     table_copy = pltpu.make_async_copy(table_any, table_ref, table_sems.at[1])
     table_copy.start()
     blocks = block_ref.shape[0]
     each = coupled // blocks
-    spread_copies = []
-    for i in range(blocks):
-        rows = pl.ds(i * each, each)
-        spread_copies.append(
-            pltpu.make_async_copy(spread_hbm.at[rows], spread_ref.at[rows], spread_sems.at[i])
-        )
-        spread_copies[-1].start()
     stride = slots * 5 // 2
     senders = recv_ref.shape[0] // stride
     left = iota((senders, LANES), 1) < HALF
@@ -159,33 +152,34 @@
         double_ref[pl.ds((slots // 2 + k) * senders, senders), :] = jnp.where(left, turned, both)
     take_copy.wait()
 
-    group = 8
-
-    for base in range(0, kept, group):
-        rows = range(base, base + group)
-        heads = [take_ref[0, j] for j in rows]
-        tails = [take_ref[1, j] for j in rows]
-        values = [
-            (recv_ref[pl.ds(h, 1), :], recv_ref[pl.ds(h + slots, 1), :], double_ref[pl.ds(t, 1), :])
-            for h, t in zip(heads, tails)
-        ]
-        for j, value in zip(rows, values):
-            for c in range(3):
-                rows_ref[c, j : j + 1, :] = value[c]
-    for c in range(3):
-        lanes = slice(c * LANES, (c + 1) * LANES)
-        high, low = split(rows_ref[c])
-        rows_high_ref[:kept, lanes] = high
-        rows_high_ref[kept:, lanes] = high
-        rows_low_ref[:, lanes] = low
+    group = 4
+    row = iota((SUB, LANES), 0)
+
+    def pick(ref, slots):
+        value = ref[pl.ds(slots[0], SUB, stride=0), :]
+        for i in range(1, SUB):
+            value = jnp.where(row == i, ref[pl.ds(slots[i], SUB, stride=0), :], value)
+        return value
+
+    for base in range(0, kept, 2 * SUB):
+        parts = []
+        for start in (base, base + SUB):
+            heads = [take_ref[0, j] for j in range(start, start + SUB)]
+            tails = [take_ref[1, j] for j in range(start, start + SUB)]
+            parts.append(
+                (pick(recv_ref, heads), pick(recv_ref, [h + slots for h in heads]), pick(double_ref, tails))
+            )
+        for c in range(3):
+            lanes = slice(c * LANES, (c + 1) * LANES)
+            high, low = split(jnp.concatenate([parts[0][c], parts[1][c]], axis=0))
+            for i, part in enumerate((high, high, low)):
+                stacked_ref[i * kept + base : i * kept + base + 2 * SUB, lanes] = part
 
     contract = ((1,), (0,))
 
     def product(i, lanes):
         rows = pl.ds(i * each, each)
-        return dot(spread_ref[rows], rows_high_ref[:, lanes], contract) + dot(
-            spread_ref[rows, :kept], rows_low_ref[:, lanes], contract
-        )
+        return dot(spread_ref[rows], stacked_ref[:, lanes], contract)
 
     oceans = head_ref.shape[0] // (2 * slots2)
 
@@ -208,17 +202,17 @@
 
     head_lanes, tail_lanes = slice(0, 2 * LANES), slice(2 * LANES, 3 * LANES)
     table_copy.wait()
-    for copy in spread_copies:
-        copy.wait()
     for i in range(blocks):
         block_ref[i] = product(i, head_lanes)
-    first = jnp.broadcast_to(block_ref[0, 0:1, :LANES], (slots2, LANES))
-    second = jnp.broadcast_to(block_ref[0, 0:1, LANES:], (slots2, LANES))
-    for o in range(oceans):
-        head_ref[2 * o * slots2 : (2 * o + 1) * slots2, :] = first
-        head_ref[(2 * o + 1) * slots2 : (2 * o + 2) * slots2, :] = second
-    for i in range(blocks):
-        scatter(i)
+        if i == 0:
+            first = jnp.broadcast_to(block_ref[0, 0:1, :LANES], (slots2, LANES))
+            second = jnp.broadcast_to(block_ref[0, 0:1, LANES:], (slots2, LANES))
+            for o in range(oceans):
+                head_ref[2 * o * slots2 : (2 * o + 1) * slots2, :] = first
+                head_ref[(2 * o + 1) * slots2 : (2 * o + 2) * slots2, :] = second
+        else:
+            scatter(i - 1)
+    scatter(blocks - 1)
     pieces = head_sems.shape[0]
     some = oceans // pieces
     copies = []
@@ -232,9 +226,11 @@
         copies[-1].start()
     for i in range(blocks):
         end_block_ref[i] = product(i, tail_lanes)
-    end_ref[...] = jnp.broadcast_to(end_block_ref[0, 0:1, :], end_ref.shape)
-    for i in range(blocks):
-        scatter_end(i)
+        if i == 0:
+            end_ref[...] = jnp.broadcast_to(end_block_ref[0, 0:1, :], end_ref.shape)
+        else:
+            scatter_end(i - 1)
+    scatter_end(blocks - 1)
     half = slots2 // 2
     left = iota((some * half, LANES), 1) < HALF
     tail_view = tail_ref.reshape(oceans, half, LANES)
@@ -365,7 +361,7 @@
     spread, take, table = pl.pallas_call(
         lambda *refs: spread_kernel(slots, *refs),
         out_shape=[
-            jax.ShapeDtypeStruct((coupled, 2 * kept), BF16),
+            jax.ShapeDtypeStruct((coupled, 3 * kept), BF16),
             jax.ShapeDtypeStruct((2, kept), I32),
             jax.ShapeDtypeStruct((2, coupled), I32),
         ],
@@ -379,29 +375,25 @@
     leaving = pl.pallas_call(
         lambda *refs: couple_kernel(slots, slots2, *refs),
         out_shape=jax.ShapeDtypeStruct((devices * wide, LANES), F32),
-        in_specs=[vmem(), vmem(), hbm(), vmem()],
+        in_specs=[vmem(), vmem(), vmem(), vmem()],
         out_specs=hbm(),
         scratch_shapes=[
             pltpu.SMEM((2, kept), I32),
             pltpu.SMEM((2, coupled), I32),
-            pltpu.VMEM((coupled, 2 * kept), BF16),
             pltpu.VMEM((devices * slots, LANES), F32),
-            pltpu.VMEM((3, kept, LANES), F32),
-            pltpu.VMEM((2 * kept, 3 * LANES), BF16),
-            pltpu.VMEM((kept, 3 * LANES), BF16),
+            pltpu.VMEM((3 * kept, 3 * LANES), BF16),
             pltpu.VMEM((devices * 2 * slots2, LANES), F32),
             pltpu.VMEM((devices * slots2 // 2, LANES), F32),
             pltpu.VMEM((devices * slots2, LANES), F32),
-            pltpu.VMEM((2, coupled // 2, 2 * LANES), F32),
-            pltpu.VMEM((2, coupled // 2, LANES), F32),
-            dma((2,)),
+            pltpu.VMEM((8, coupled // 8, 2 * LANES), F32),
+            pltpu.VMEM((8, coupled // 8, LANES), F32),
             dma((2,)),
             dma((4,)),
             dma((4,)),
         ],
-        compiler_params=params(51),
+        compiler_params=params(24),
         name="couple",
-    )(take, table, in_hbm(spread), received)
+    )(take, table, spread, received)
     arrived = exchange(leaving, devices)
 
     base = (ocean_from // slots2) * wide

time: 86.8 us -> 89 us (1.025)
  local copies, waits for them, and re-layouts: 1.36 us -> 5.04 us
  Pallas kernels: 18.2 us -> 16.8 us
    unnamed x14 -> x18, local copies, waits for them, and re-layouts: 1.36 us -> 5.04 us
    pallas_call x1, Pallas kernels: 5.92 us -> 4.56 us  [shards(): pl.pallas_call(lambda *refs: couple_kernel(slots, slots2, *refs), out_sha...]
  transfers between devices with their start and end apart: 2 -> 2, of which waited for: 2 -> 2; matrix products, arithmetic and copies ran while one was open for 0% -> 0% of each run, Pallas kernels for 8% -> 7%
where the time goes in v5:
time: 89 us; the launch traced here: 88.6 us
  waiting for transfers between devices  50 us (56%)
  Pallas kernels  16.8 us (19%)
  starting transfers between devices  16 us (18%)
  local copies, waits for them, and re-layouts  5.04 us (6%)
    all_to_all x2, waiting for transfers between devices, exchange(): lax.all_to_all(shaped, 'comp', split_axis=0, concat_axis=0, tiled=True)  50 us
    all_to_all x2, starting transfers between devices, exchange(): lax.all_to_all(shaped, 'comp', split_axis=0, concat_axis=0, tiled=True)  16 us
    pallas_call x1, Pallas kernels, shards(): pl.pallas_call(lambda *refs: spread_kernel(slots, *refs), out_shape=[jax....  6.54 us
    unnamed x18, local copies, waits for them, and re-layouts  5.04 us
    pallas_call x1, Pallas kernels, shards(): pl.pallas_call(lambda *refs: couple_kernel(slots, slots2, *refs), out_sha...  4.56 us
    pallas_call x1, Pallas kernels, shards(): pl.pallas_call(lambda *refs: place_kernel(slots2, *refs), out_shape=[jax....  2.98 us
    pallas_call x1, Pallas kernels, shards(): pl.pallas_call(gather_kernel, out_shape=jax.ShapeDtypeStruct((devices * n...  2.76 us
  transfers between devices with their start and end apart: 2, of which 2 were waited for; matrix products, arithmetic and copies ran while one was open for 0% of the time, Pallas kernels for 7%

profile of v5, /device:TPU:1, one launch (start us, length us, event | category | flops | bytes accessed | tf_op | source)
XLA Modules:
  0.0 88.6 jit_solution(10736596194598483103)
XLA Ops:
  0.6 0.0 copy-start.3
  0.6 0.0 copy-start.4
  0.7 0.0 copy-start.5
  0.7 2.8 %gather_rows.1 = f32[2560,128]{1,0:T(8,128)} custom-call(s32[8,128]{1,0:T(8,128)} %bitcast.21, f32[320,256]{1,0:T(8,128)} %bitcast.18), custom_call_target="tpu_custom_call" | custom-call | tf_op jit(solution)/shard_map/gather_rows/pallas_call | solution.py:343
  3.4 11.5 %all-to-all-start = ((f32[128,5,4,128]{3,2,1,0:T(4,128)}), f32[128,5,4,128]{3,2,1,0:T(4,128)S(1)}, u32[]{:S(2)}, u32[]{:S(2)}) async-start(f32[128,5,4,128]{3,2,1,0:T(4,128)} %bitcast.7), calls=%async_computation | async-start | bytes 2621440 | tf_op jit(solution)/shard_map/all_to_all | solution.py:326
  14.9 0.0 copy-done.3
  15.0 0.0 copy-done.4
  15.0 0.0 copy-done.5
  15.0 6.5 %spread_weights.1 = (bf16[1024,1536]{1,0:T(8,128)(2,1)S(1)}, s32[2,512]{1,0:T(2,128)S(1)}, s32[2,1024]{1,0:T(2,128)S(1)}) custom-call(s32[4,512]{1,0:T(4,128)S(1)} %copy-done.4, f32[4,256,512]{2,1,0:T(8,128)S(1)} %copy-done.3, s32[16,128]{1,0:T(8,128)S(1)} %bitcast.16), custom_call_target="tpu_custom_call" | custom-call | tf_op jit(solution)/shard_map/spread_weights/pallas_call | solution.py:361
  21.5 0.0 copy-start.1
  21.5 1.6 %copy-done.1 = bf16[1024,1536]{1,0:T(8,128)(2,1)} copy-done((bf16[1024,1536]{1,0:T(8,128)(2,1)}, bf16[1024,1536]{1,0:T(8,128)(2,1)S(1)}, u32[]{:S(2)}) %copy-start.1) | copy-done | bytes 3145752
  23.2 13.9 %all-to-all-done = f32[128,5,4,128]{3,2,1,0:T(4,128)S(1)} async-done(((f32[128,5,4,128]{3,2,1,0:T(4,128)}), f32[128,5,4,128]{3,2,1,0:T(4,128)S(1)}, u32[]{:S(2)}, u32[]{:S(2)}) %all-to-all-start) | async-done | bytes 1310752 | tf_op jit(solution)/shard_map/all_to_all | solution.py:326
  37.1 0.0 copy-start.2
  37.1 1.9 %copy-done.2 = bf16[1024,1536]{1,0:T(8,128)(2,1)S(1)} copy-done((bf16[1024,1536]{1,0:T(8,128)(2,1)S(1)}, bf16[1024,1536]{1,0:T(8,128)(2,1)}, u32[]{:S(2)}) %copy-start.2) | copy-done | bytes 3145752
  39.0 4.6 %couple.1 = f32[5120,128]{1,0:T(8,128)S(1)} custom-call(s32[2,512]{1,0:T(2,128)S(1)} %get-tuple-element.7.refs_0_, s32[2,1024]{1,0:T(2,128)S(1)} %get-tuple-element.8.refs_1_, bf16[1024,1536]{1,0:T(8,128)(2,1)S(1)} %copy-done.2, f32[2560,128]{1,0:T(8,128)S(1)} %bitcast.14), custom_call_target="tpu_custom_call" | custom-call | tf_op jit(solution)/shard_map/couple/pallas_call | solution.py:375
  43.6 0.0 copy-start
  43.6 1.5 %copy-done = f32[5120,128]{1,0:T(8,128)} copy-done((f32[5120,128]{1,0:T(8,128)}, f32[5120,128]{1,0:T(8,128)S(1)}, u32[]{:S(2)}) %copy-start) | copy-done | bytes 2621464
  45.1 0.0 copy-start.8
  45.1 0.0 copy-start.6
  45.1 0.0 copy-start.7
  45.1 4.5 %all-to-all-start.1 = ((f32[128,10,4,128]{3,2,1,0:T(4,128)}), f32[128,10,4,128]{3,2,1,0:T(4,128)S(1)}, u32[]{:S(2)}, u32[]{:S(2)}) async-start(f32[128,10,4,128]{3,2,1,0:T(4,128)} %bitcast.13), calls=%async_computation.1 | async-start | bytes 5242880 | tf_op jit(solution)/shard_map/all_to_all | solution.py:326
  49.5 0.0 copy-done.8
  49.6 36.1 %all-to-all-done.1 = f32[128,10,4,128]{3,2,1,0:T(4,128)S(1)} async-done(((f32[128,10,4,128]{3,2,1,0:T(4,128)}), f32[128,10,4,128]{3,2,1,0:T(4,128)S(1)}, u32[]{:S(2)}, u32[]{:S(2)}) %all-to-all-start.1) | async-done | bytes 2621472 | tf_op jit(solution)/shard_map/all_to_all | solution.py:326
  85.7 0.0 copy-done.6
  85.7 0.0 copy-done.7
  85.7 3.0 %place.1 = (f32[320,1024]{1,0:T(8,128)}, f32[4,1024]{1,0:T(4,128)}) custom-call(s32[2,1024]{1,0:T(2,128)S(1)} %pad_add_fusion.refs_0_, s32[1,1024]{1,0:T(1,128)S(1)} %bitcast.15, f32[1,1024]{1,0:T(1,128)S(1)} %bitcast.17, f32[2,1024]{1,0:T(2,128)S(1)} %copy-done.6, f32[5120,128]{1,0:T(8,128)S(1)} %bitcast.12), custom_call_target="tpu_custom_call" | custom-call | tf_op jit(solution)/shard_map/place/pallas_call | solution.py:405
  (3 shorter events, 0.0 us)
Async XLA Ops:
  0.6 14.3 %copy-start.3 = (f32[4,256,512]{2,1,0:T(8,128)S(1)}, f32[4,256,512]{2,1,0:T(8,128)}, u32[]{:S(2)}) copy-start(f32[4,256,512]{2,1,0:T(8,128)} %refs_1_.1) | copy-start | bytes 6291460
  0.6 14.3 %copy-start.4 = (s32[4,512]{1,0:T(4,128)S(1)}, s32[4,512]{1,0:T(4,128)}, u32[]{:S(2)}) copy-start(s32[4,512]{1,0:T(4,128)} %refs_0_.1) | copy-start | bytes 24580
  0.7 14.3 %copy-start.5 = (s32[128,16]{0,1:T(8,128)S(1)}, s32[128,16]{0,1:T(8,128)}, u32[]{:S(2)}) copy-start(s32[128,16]{0,1:T(8,128)} %param.12) | copy-start | bytes 24580
  3.4 33.7 %all-to-all-start = ((f32[128,5,4,128]{3,2,1,0:T(4,128)}), f32[128,5,4,128]{3,2,1,0:T(4,128)S(1)}, u32[]{:S(2)}, u32[]{:S(2)}) async-start(f32[128,5,4,128]{3,2,1,0:T(4,128)} %bitcast.7), calls=%async_computation | async-start | bytes 2621440 | tf_op jit(solution)/shard_map/all_to_all | solution.py:326
  21.5 1.6 %copy-start.1 = (bf16[1024,1536]{1,0:T(8,128)(2,1)}, bf16[1024,1536]{1,0:T(8,128)(2,1)S(1)}, u32[]{:S(2)}) copy-start(bf16[1024,1536]{1,0:T(8,128)(2,1)S(1)} %get-tuple-element.9.refs_2_) | copy-start | bytes 9437188
  37.1 1.9 %copy-start.2 = (bf16[1024,1536]{1,0:T(8,128)(2,1)S(1)}, bf16[1024,1536]{1,0:T(8,128)(2,1)}, u32[]{:S(2)}) copy-start(bf16[1024,1536]{1,0:T(8,128)(2,1)} %copy-done.1) | copy-start | bytes 9437188
  43.6 1.5 %copy-start = (f32[5120,128]{1,0:T(8,128)}, f32[5120,128]{1,0:T(8,128)S(1)}, u32[]{:S(2)}) copy-start(f32[5120,128]{1,0:T(8,128)S(1)} %couple.1) | copy-start | bytes 7864324
  45.1 4.5 %copy-start.8 = (s32[1024]{0:T(1024)S(1)}, s32[1024]{0:T(1024)}, u32[]{:S(2)}) copy-start(s32[1024]{0:T(1024)} %param.13) | copy-start | bytes 12292
  45.1 40.6 %copy-start.6 = (f32[2,1024]{1,0:T(2,128)S(1)}, f32[2,1024]{1,0:T(2,128)}, u32[]{:S(2)}) copy-start(f32[2,1024]{1,0:T(2,128)} %refs_3_.1) | copy-start | bytes 24580
  45.1 40.6 %copy-start.7 = (f32[1024]{0:T(1024)S(1)}, f32[1024]{0:T(1024)}, u32[]{:S(2)}) copy-start(f32[1024]{0:T(1024)} %param.14) | copy-start | bytes 12292
  45.1 40.6 %all-to-all-start.1 = ((f32[128,10,4,128]{3,2,1,0:T(4,128)}), f32[128,10,4,128]{3,2,1,0:T(4,128)S(1)}, u32[]{:S(2)}, u32[]{:S(2)}) async-start(f32[128,10,4,128]{3,2,1,0:T(4,128)} %bitcast.13), calls=%async_computation.1 | async-start | bytes 5242880 | tf_op jit(solution)/shard_map/all_to_all | solution.py:326

commit v6 on v5

--- a/solution.py
+++ b/solution.py
@@ -83,7 +83,7 @@
 
 def spread_kernel(slots, src_ref, weights_ref, send_ref, spread_ref, take_ref, table_ref, hot_ref):
     blocks, block_rows, block_cols = weights_ref.shape
-    coupled, kept = spread_ref.shape[0], spread_ref.shape[1] // 3
+    coupled, kept = spread_ref.shape[0], spread_ref.shape[1] // 2
     total = hot_ref.shape[1]
     senders = total // slots
     counts = jnp.zeros((SUB, total), F32)
@@ -102,7 +102,7 @@
         high, low = split(weights_ref[b])
         summed = dot(high, hot, ((1,), (1,))) + dot(low, hot, ((1,), (1,)))
         high, low = split(summed)
-        for i, part in enumerate((high, low, high)):
+        for i, part in enumerate((high, low)):
             spread_ref[b * block_rows : (b + 1) * block_rows, i * kept : (i + 1) * kept] = part
 
     slot = iota((SUB, total), 1)
@@ -135,7 +135,7 @@
     take_ref, table_ref, double_ref, stacked_ref,
     head_ref, tail_ref, end_ref, block_ref, end_block_ref, table_sems, head_sems, tail_sems,
 ):
-    coupled, kept = spread_ref.shape[0], spread_ref.shape[1] // 3
+    coupled, kept = spread_ref.shape[0], spread_ref.shape[1] // 2
     take_copy = pltpu.make_async_copy(take_any, take_ref, table_sems.at[0])
     take_copy.start()
     table_copy = pltpu.make_async_copy(table_any, table_ref, table_sems.at[1])
@@ -179,7 +179,9 @@
 
     def product(i, lanes):
         rows = pl.ds(i * each, each)
-        return dot(spread_ref[rows], stacked_ref[:, lanes], contract)
+        return dot(spread_ref[rows], stacked_ref[: 2 * kept, lanes], contract) + dot(
+            spread_ref[rows, :kept], stacked_ref[2 * kept :, lanes], contract
+        )
 
     oceans = head_ref.shape[0] // (2 * slots2)
 
@@ -361,7 +363,7 @@
     spread, take, table = pl.pallas_call(
         lambda *refs: spread_kernel(slots, *refs),
         out_shape=[
-            jax.ShapeDtypeStruct((coupled, 3 * kept), BF16),
+            jax.ShapeDtypeStruct((coupled, 2 * kept), BF16),
             jax.ShapeDtypeStruct((2, kept), I32),
             jax.ShapeDtypeStruct((2, coupled), I32),
         ],

time: 89 us -> 86.4 us (0.971)
  local copies, waits for them, and re-layouts: 5.04 us -> 1.61 us
  Pallas kernels: 16.8 us -> 17.7 us
    unnamed x18 -> x12, local copies, waits for them, and re-layouts: 5.04 us -> 1.61 us
    pallas_call x1, Pallas kernels: 4.56 us -> 5.54 us  [shards(): pl.pallas_call(lambda *refs: couple_kernel(slots, slots2, *refs), out_sha...]
  transfers between devices with their start and end apart: 2 -> 2, of which waited for: 2 -> 2; matrix products, arithmetic and copies ran while one was open for 0% -> 0% of each run, Pallas kernels for 7% -> 8%
where the time goes in v6:
time: 86.4 us; the launch traced here: 86 us
  waiting for transfers between devices  50.1 us (58%)
  Pallas kernels  17.7 us (20%)
  starting transfers between devices  15.8 us (18%)
  local copies, waits for them, and re-layouts  1.61 us (2%)
    all_to_all x2, waiting for transfers between devices, exchange(): lax.all_to_all(shaped, 'comp', split_axis=0, concat_axis=0, tiled=True)  50.1 us
    all_to_all x2, starting transfers between devices, exchange(): lax.all_to_all(shaped, 'comp', split_axis=0, concat_axis=0, tiled=True)  15.8 us
    pallas_call x1, Pallas kernels, shards(): pl.pallas_call(lambda *refs: spread_kernel(slots, *refs), out_shape=[jax....  6.51 us
    pallas_call x1, Pallas kernels, shards(): pl.pallas_call(lambda *refs: couple_kernel(slots, slots2, *refs), out_sha...  5.54 us
    pallas_call x1, Pallas kernels, shards(): pl.pallas_call(lambda *refs: place_kernel(slots2, *refs), out_shape=[jax....  2.98 us
    pallas_call x1, Pallas kernels, shards(): pl.pallas_call(gather_kernel, out_shape=jax.ShapeDtypeStruct((devices * n...  2.63 us
  transfers between devices with their start and end apart: 2, of which 2 were waited for; matrix products, arithmetic and copies ran while one was open for 0% of the time, Pallas kernels for 8%

profile of v6, /device:TPU:1, one launch (start us, length us, event | category | flops | bytes accessed | tf_op | source)
XLA Modules:
  0.0 86.0 jit_solution(11873059131460591920)
XLA Ops:
  0.6 0.0 copy-start.1
  0.6 0.0 copy-start.2
  0.7 2.6 %gather_rows.1 = f32[2560,128]{1,0:T(8,128)} custom-call(s32[8,128]{1,0:T(8,128)} %bitcast.20, f32[320,256]{1,0:T(8,128)} %bitcast.17), custom_call_target="tpu_custom_call" | custom-call | tf_op jit(solution)/shard_map/gather_rows/pallas_call | solution.py:345
  3.3 11.5 %all-to-all-start = ((f32[128,5,4,128]{3,2,1,0:T(4,128)}), f32[128,5,4,128]{3,2,1,0:T(4,128)S(1)}, u32[]{:S(2)}, u32[]{:S(2)}) async-start(f32[128,5,4,128]{3,2,1,0:T(4,128)} %bitcast.7), calls=%async_computation | async-start | bytes 2621440 | tf_op jit(solution)/shard_map/all_to_all | solution.py:328
  14.8 0.0 copy-done.1
  14.8 0.0 copy-done.2
  14.8 0.0 copy-start
  14.8 1.6 %copy-done = f32[4,256,512]{2,1,0:T(8,128)S(1)} copy-done((f32[4,256,512]{2,1,0:T(8,128)S(1)}, f32[4,256,512]{2,1,0:T(8,128)}, u32[]{:S(2)}) %copy-start) | copy-done | bytes 2097176
  16.4 6.5 %spread_weights.1 = (bf16[1024,1024]{1,0:T(8,128)(2,1)S(1)}, s32[2,512]{1,0:T(2,128)S(1)}, s32[2,1024]{1,0:T(2,128)S(1)}) custom-call(s32[4,512]{1,0:T(4,128)S(1)} %copy-done.1, f32[4,256,512]{2,1,0:T(8,128)S(1)} %copy-done, s32[16,128]{1,0:T(8,128)S(1)} %bitcast.15), custom_call_target="tpu_custom_call" | custom-call | tf_op jit(solution)/shard_map/spread_weights/pallas_call | solution.py:363
  22.9 14.0 %all-to-all-done = f32[128,5,4,128]{3,2,1,0:T(4,128)S(1)} async-done(((f32[128,5,4,128]{3,2,1,0:T(4,128)}), f32[128,5,4,128]{3,2,1,0:T(4,128)S(1)}, u32[]{:S(2)}, u32[]{:S(2)}) %all-to-all-start) | async-done | bytes 1310752 | tf_op jit(solution)/shard_map/all_to_all | solution.py:328
  37.0 5.5 %couple.1 = f32[5120,128]{1,0:T(8,128)} custom-call(s32[2,512]{1,0:T(2,128)S(1)} %get-tuple-element.7.refs_0_, s32[2,1024]{1,0:T(2,128)S(1)} %get-tuple-element.8.refs_1_, bf16[1024,1024]{1,0:T(8,128)(2,1)S(1)} %get-tuple-element.9.refs_2_, f32[2560,128]{1,0:T(8,128)S(1)} %bitcast.13), custom_call_target="tpu_custom_call" | custom-call | tf_op jit(solution)/shard_map/couple/pallas_call | solution.py:377
  42.5 0.0 copy-start.5
  42.5 0.0 copy-start.3
  42.5 0.0 copy-start.4
  42.5 4.3 %all-to-all-start.1 = ((f32[128,10,4,128]{3,2,1,0:T(4,128)}), f32[128,10,4,128]{3,2,1,0:T(4,128)S(1)}, u32[]{:S(2)}, u32[]{:S(2)}) async-start(f32[128,10,4,128]{3,2,1,0:T(4,128)} %bitcast.9), calls=%async_computation.1 | async-start | bytes 5242880 | tf_op jit(solution)/shard_map/all_to_all | solution.py:328
  46.9 0.0 copy-done.5
  47.0 36.1 %all-to-all-done.1 = f32[128,10,4,128]{3,2,1,0:T(4,128)S(1)} async-done(((f32[128,10,4,128]{3,2,1,0:T(4,128)}), f32[128,10,4,128]{3,2,1,0:T(4,128)S(1)}, u32[]{:S(2)}, u32[]{:S(2)}) %all-to-all-start.1) | async-done | bytes 2621472 | tf_op jit(solution)/shard_map/all_to_all | solution.py:328
  83.0 0.0 copy-done.3
  83.0 0.0 copy-done.4
  83.0 3.0 %place.1 = (f32[320,1024]{1,0:T(8,128)}, f32[4,1024]{1,0:T(4,128)}) custom-call(s32[2,1024]{1,0:T(2,128)S(1)} %pad_add_fusion.refs_0_, s32[1,1024]{1,0:T(1,128)S(1)} %bitcast.14, f32[1,1024]{1,0:T(1,128)S(1)} %bitcast.16, f32[2,1024]{1,0:T(2,128)S(1)} %copy-done.3, f32[5120,128]{1,0:T(8,128)S(1)} %bitcast.12), custom_call_target="tpu_custom_call" | custom-call | tf_op jit(solution)/shard_map/place/pallas_call | solution.py:407
  (3 shorter events, 0.0 us)
Async XLA Ops:
  0.6 14.2 %copy-start.1 = (s32[4,512]{1,0:T(4,128)S(1)}, s32[4,512]{1,0:T(4,128)}, u32[]{:S(2)}) copy-start(s32[4,512]{1,0:T(4,128)} %refs_0_.1) | copy-start | bytes 24580
  0.6 14.2 %copy-start.2 = (s32[128,16]{0,1:T(8,128)S(1)}, s32[128,16]{0,1:T(8,128)}, u32[]{:S(2)}) copy-start(s32[128,16]{0,1:T(8,128)} %param.12) | copy-start | bytes 24580
  3.3 33.7 %all-to-all-start = ((f32[128,5,4,128]{3,2,1,0:T(4,128)}), f32[128,5,4,128]{3,2,1,0:T(4,128)S(1)}, u32[]{:S(2)}, u32[]{:S(2)}) async-start(f32[128,5,4,128]{3,2,1,0:T(4,128)} %bitcast.7), calls=%async_computation | async-start | bytes 2621440 | tf_op jit(solution)/shard_map/all_to_all | solution.py:328
  14.8 1.6 %copy-start = (f32[4,256,512]{2,1,0:T(8,128)S(1)}, f32[4,256,512]{2,1,0:T(8,128)}, u32[]{:S(2)}) copy-start(f32[4,256,512]{2,1,0:T(8,128)} %refs_1_.1) | copy-start | bytes 6291460
  42.5 4.4 %copy-start.5 = (s32[1024]{0:T(1024)S(1)}, s32[1024]{0:T(1024)}, u32[]{:S(2)}) copy-start(s32[1024]{0:T(1024)} %param.13) | copy-start | bytes 12292
  42.5 40.5 %copy-start.3 = (f32[2,1024]{1,0:T(2,128)S(1)}, f32[2,1024]{1,0:T(2,128)}, u32[]{:S(2)}) copy-start(f32[2,1024]{1,0:T(2,128)} %refs_3_.1) | copy-start | bytes 24580
  42.5 40.5 %copy-start.4 = (f32[1024]{0:T(1024)S(1)}, f32[1024]{0:T(1024)}, u32[]{:S(2)}) copy-start(f32[1024]{0:T(1024)} %param.14) | copy-start | bytes 12292
  42.5 40.5 %all-to-all-start.1 = ((f32[128,10,4,128]{3,2,1,0:T(4,128)}), f32[128,10,4,128]{3,2,1,0:T(4,128)S(1)}, u32[]{:S(2)}, u32[]{:S(2)}) async-start(f32[128,10,4,128]{3,2,1,0:T(4,128)} %bitcast.9), calls=%async_computation.1 | async-start | bytes 5242880 | tf_op jit(solution)/shard_map/all_to_all | solution.py:328

commit v7 on v6

--- a/solution.py
+++ b/solution.py
@@ -288,7 +288,7 @@
         flux_ref[3:4, lanes] = scale * (wind_north - current_ref[1:2, lanes])
 
     copies = []
-    phases = 2
+    phases = 4
     for phase in range(phases):
         some = range(phase * blocks // phases, (phase + 1) * blocks // phases)
         for b in some:
@@ -351,7 +351,7 @@
             pltpu.VMEM((slots, devices), I32),
             pltpu.VMEM((columns, rows), F32),
             pltpu.VMEM((devices * narrow, LANES), F32),
-            dma((5,)),
+            dma((2,)),
             dma((4,)),
         ],
         compiler_params=params(16),

time: 86.4 us -> 86.2 us (level)
  no operation moved by 1% of the time
where the time goes in v7:
time: 86.2 us; the launch traced here: 85.9 us
  waiting for transfers between devices  50.1 us (58%)
  Pallas kernels  17.6 us (20%)
  starting transfers between devices  15.8 us (18%)
  local copies, waits for them, and re-layouts  1.61 us (2%)
    all_to_all x2, waiting for transfers between devices, exchange(): lax.all_to_all(shaped, 'comp', split_axis=0, concat_axis=0, tiled=True)  50.1 us
    all_to_all x2, starting transfers between devices, exchange(): lax.all_to_all(shaped, 'comp', split_axis=0, concat_axis=0, tiled=True)  15.8 us
    pallas_call x1, Pallas kernels, shards(): pl.pallas_call(lambda *refs: spread_kernel(slots, *refs), out_shape=[jax....  6.54 us
    pallas_call x1, Pallas kernels, shards(): pl.pallas_call(lambda *refs: couple_kernel(slots, slots2, *refs), out_sha...  5.54 us
    pallas_call x1, Pallas kernels, shards(): pl.pallas_call(lambda *refs: place_kernel(slots2, *refs), out_shape=[jax....  2.89 us
    pallas_call x1, Pallas kernels, shards(): pl.pallas_call(gather_kernel, out_shape=jax.ShapeDtypeStruct((devices * n...  2.6 us
  transfers between devices with their start and end apart: 2, of which 2 were waited for; matrix products, arithmetic and copies ran while one was open for 0% of the time, Pallas kernels for 8%

profile of v7, /device:TPU:1, one launch (start us, length us, event | category | flops | bytes accessed | tf_op | source)
XLA Modules:
  0.0 85.9 jit_solution(10521765884796859475)
XLA Ops:
  0.6 0.0 copy-start.1
  0.6 0.0 copy-start.2
  0.7 2.6 %gather_rows.1 = f32[2560,128]{1,0:T(8,128)} custom-call(s32[8,128]{1,0:T(8,128)} %bitcast.20, f32[320,256]{1,0:T(8,128)} %bitcast.17), custom_call_target="tpu_custom_call" | custom-call | tf_op jit(solution)/shard_map/gather_rows/pallas_call | solution.py:345
  3.3 11.5 %all-to-all-start = ((f32[128,5,4,128]{3,2,1,0:T(4,128)}), f32[128,5,4,128]{3,2,1,0:T(4,128)S(1)}, u32[]{:S(2)}, u32[]{:S(2)}) async-start(f32[128,5,4,128]{3,2,1,0:T(4,128)} %bitcast.7), calls=%async_computation | async-start | bytes 2621440 | tf_op jit(solution)/shard_map/all_to_all | solution.py:328
  14.8 0.0 copy-done.1
  14.8 0.0 copy-done.2
  14.8 0.0 copy-start
  14.8 1.6 %copy-done = f32[4,256,512]{2,1,0:T(8,128)S(1)} copy-done((f32[4,256,512]{2,1,0:T(8,128)S(1)}, f32[4,256,512]{2,1,0:T(8,128)}, u32[]{:S(2)}) %copy-start) | copy-done | bytes 2097176
  16.4 6.5 %spread_weights.1 = (bf16[1024,1024]{1,0:T(8,128)(2,1)S(1)}, s32[2,512]{1,0:T(2,128)S(1)}, s32[2,1024]{1,0:T(2,128)S(1)}) custom-call(s32[4,512]{1,0:T(4,128)S(1)} %copy-done.1, f32[4,256,512]{2,1,0:T(8,128)S(1)} %copy-done, s32[16,128]{1,0:T(8,128)S(1)} %bitcast.15), custom_call_target="tpu_custom_call" | custom-call | tf_op jit(solution)/shard_map/spread_weights/pallas_call | solution.py:363
  22.9 14.0 %all-to-all-done = f32[128,5,4,128]{3,2,1,0:T(4,128)S(1)} async-done(((f32[128,5,4,128]{3,2,1,0:T(4,128)}), f32[128,5,4,128]{3,2,1,0:T(4,128)S(1)}, u32[]{:S(2)}, u32[]{:S(2)}) %all-to-all-start) | async-done | bytes 1310752 | tf_op jit(solution)/shard_map/all_to_all | solution.py:328
  36.9 5.5 %couple.1 = f32[5120,128]{1,0:T(8,128)} custom-call(s32[2,512]{1,0:T(2,128)S(1)} %get-tuple-element.7.refs_0_, s32[2,1024]{1,0:T(2,128)S(1)} %get-tuple-element.8.refs_1_, bf16[1024,1024]{1,0:T(8,128)(2,1)S(1)} %get-tuple-element.9.refs_2_, f32[2560,128]{1,0:T(8,128)S(1)} %bitcast.13), custom_call_target="tpu_custom_call" | custom-call | tf_op jit(solution)/shard_map/couple/pallas_call | solution.py:377
  42.5 0.0 copy-start.5
  42.5 0.0 copy-start.3
  42.5 0.0 copy-start.4
  42.5 4.3 %all-to-all-start.1 = ((f32[128,10,4,128]{3,2,1,0:T(4,128)}), f32[128,10,4,128]{3,2,1,0:T(4,128)S(1)}, u32[]{:S(2)}, u32[]{:S(2)}) async-start(f32[128,10,4,128]{3,2,1,0:T(4,128)} %bitcast.9), calls=%async_computation.1 | async-start | bytes 5242880 | tf_op jit(solution)/shard_map/all_to_all | solution.py:328
  46.9 0.0 copy-done.5
  46.9 36.1 %all-to-all-done.1 = f32[128,10,4,128]{3,2,1,0:T(4,128)S(1)} async-done(((f32[128,10,4,128]{3,2,1,0:T(4,128)}), f32[128,10,4,128]{3,2,1,0:T(4,128)S(1)}, u32[]{:S(2)}, u32[]{:S(2)}) %all-to-all-start.1) | async-done | bytes 2621472 | tf_op jit(solution)/shard_map/all_to_all | solution.py:328
  83.0 0.0 copy-done.3
  83.0 0.0 copy-done.4
  83.0 2.9 %place.1 = (f32[320,1024]{1,0:T(8,128)}, f32[4,1024]{1,0:T(4,128)}) custom-call(s32[2,1024]{1,0:T(2,128)S(1)} %pad_add_fusion.refs_0_, s32[1,1024]{1,0:T(1,128)S(1)} %bitcast.14, f32[1,1024]{1,0:T(1,128)S(1)} %bitcast.16, f32[2,1024]{1,0:T(2,128)S(1)} %copy-done.3, f32[5120,128]{1,0:T(8,128)S(1)} %bitcast.12), custom_call_target="tpu_custom_call" | custom-call | tf_op jit(solution)/shard_map/place/pallas_call | solution.py:407
  (3 shorter events, 0.0 us)
Async XLA Ops:
  0.6 14.1 %copy-start.1 = (s32[4,512]{1,0:T(4,128)S(1)}, s32[4,512]{1,0:T(4,128)}, u32[]{:S(2)}) copy-start(s32[4,512]{1,0:T(4,128)} %refs_0_.1) | copy-start | bytes 24580
  0.6 14.1 %copy-start.2 = (s32[128,16]{0,1:T(8,128)S(1)}, s32[128,16]{0,1:T(8,128)}, u32[]{:S(2)}) copy-start(s32[128,16]{0,1:T(8,128)} %param.12) | copy-start | bytes 24580
  3.3 33.7 %all-to-all-start = ((f32[128,5,4,128]{3,2,1,0:T(4,128)}), f32[128,5,4,128]{3,2,1,0:T(4,128)S(1)}, u32[]{:S(2)}, u32[]{:S(2)}) async-start(f32[128,5,4,128]{3,2,1,0:T(4,128)} %bitcast.7), calls=%async_computation | async-start | bytes 2621440 | tf_op jit(solution)/shard_map/all_to_all | solution.py:328
  14.8 1.6 %copy-start = (f32[4,256,512]{2,1,0:T(8,128)S(1)}, f32[4,256,512]{2,1,0:T(8,128)}, u32[]{:S(2)}) copy-start(f32[4,256,512]{2,1,0:T(8,128)} %refs_1_.1) | copy-start | bytes 6291460
  42.5 4.4 %copy-start.5 = (s32[1024]{0:T(1024)S(1)}, s32[1024]{0:T(1024)}, u32[]{:S(2)}) copy-start(s32[1024]{0:T(1024)} %param.13) | copy-start | bytes 12292
  42.5 40.5 %copy-start.3 = (f32[2,1024]{1,0:T(2,128)S(1)}, f32[2,1024]{1,0:T(2,128)}, u32[]{:S(2)}) copy-start(f32[2,1024]{1,0:T(2,128)} %refs_3_.1) | copy-start | bytes 24580
  42.5 40.5 %copy-start.4 = (f32[1024]{0:T(1024)S(1)}, f32[1024]{0:T(1024)}, u32[]{:S(2)}) copy-start(f32[1024]{0:T(1024)} %param.14) | copy-start | bytes 12292
  42.5 40.5 %all-to-all-start.1 = ((f32[128,10,4,128]{3,2,1,0:T(4,128)}), f32[128,10,4,128]{3,2,1,0:T(4,128)S(1)}, u32[]{:S(2)}, u32[]{:S(2)}) async-start(f32[128,10,4,128]{3,2,1,0:T(4,128)} %bitcast.9), calls=%async_computation.1 | async-start | bytes 5242880 | tf_op jit(solution)/shard_map/all_to_all | solution.py:328

commit v8 on v7

--- a/solution.py
+++ b/solution.py
@@ -288,7 +288,7 @@
         flux_ref[3:4, lanes] = scale * (wind_north - current_ref[1:2, lanes])
 
     copies = []
-    phases = 4
+    phases = 8
     for phase in range(phases):
         some = range(phase * blocks // phases, (phase + 1) * blocks // phases)
         for b in some:

time: 86.2 us -> 86.2 us (level)
  no operation moved by 1% of the time
where the time goes in v8:
time: 86.2 us; the launch traced here: 85.8 us
  waiting for transfers between devices  50.1 us (58%)
  Pallas kernels  17.5 us (20%)
  starting transfers between devices  15.9 us (18%)
  local copies, waits for them, and re-layouts  1.61 us (2%)
    all_to_all x2, waiting for transfers between devices, exchange(): lax.all_to_all(shaped, 'comp', split_axis=0, concat_axis=0, tiled=True)  50.1 us
    all_to_all x2, starting transfers between devices, exchange(): lax.all_to_all(shaped, 'comp', split_axis=0, concat_axis=0, tiled=True)  15.9 us
    pallas_call x1, Pallas kernels, shards(): pl.pallas_call(lambda *refs: spread_kernel(slots, *refs), out_shape=[jax....  6.54 us
    pallas_call x1, Pallas kernels, shards(): pl.pallas_call(lambda *refs: couple_kernel(slots, slots2, *refs), out_sha...  5.54 us
    pallas_call x1, Pallas kernels, shards(): pl.pallas_call(lambda *refs: place_kernel(slots2, *refs), out_shape=[jax....  2.83 us
    pallas_call x1, Pallas kernels, shards(): pl.pallas_call(gather_kernel, out_shape=jax.ShapeDtypeStruct((devices * n...  2.6 us
  transfers between devices with their start and end apart: 2, of which 2 were waited for; matrix products, arithmetic and copies ran while one was open for 0% of the time, Pallas kernels for 8%

profile of v8, /device:TPU:1, one launch (start us, length us, event | category | flops | bytes accessed | tf_op | source)
XLA Modules:
  0.0 85.8 jit_solution(12523208974902410418)
XLA Ops:
  0.6 0.0 copy-start.1
  0.6 0.0 copy-start.2
  0.7 2.6 %gather_rows.1 = f32[2560,128]{1,0:T(8,128)} custom-call(s32[8,128]{1,0:T(8,128)} %bitcast.20, f32[320,256]{1,0:T(8,128)} %bitcast.17), custom_call_target="tpu_custom_call" | custom-call | tf_op jit(solution)/shard_map/gather_rows/pallas_call | solution.py:345
  3.3 11.5 %all-to-all-start = ((f32[128,5,4,128]{3,2,1,0:T(4,128)}), f32[128,5,4,128]{3,2,1,0:T(4,128)S(1)}, u32[]{:S(2)}, u32[]{:S(2)}) async-start(f32[128,5,4,128]{3,2,1,0:T(4,128)} %bitcast.7), calls=%async_computation | async-start | bytes 2621440 | tf_op jit(solution)/shard_map/all_to_all | solution.py:328
  14.8 0.0 copy-done.1
  14.8 0.0 copy-done.2
  14.8 0.0 copy-start
  14.8 1.6 %copy-done = f32[4,256,512]{2,1,0:T(8,128)S(1)} copy-done((f32[4,256,512]{2,1,0:T(8,128)S(1)}, f32[4,256,512]{2,1,0:T(8,128)}, u32[]{:S(2)}) %copy-start) | copy-done | bytes 2097176
  16.4 6.5 %spread_weights.1 = (bf16[1024,1024]{1,0:T(8,128)(2,1)S(1)}, s32[2,512]{1,0:T(2,128)S(1)}, s32[2,1024]{1,0:T(2,128)S(1)}) custom-call(s32[4,512]{1,0:T(4,128)S(1)} %copy-done.1, f32[4,256,512]{2,1,0:T(8,128)S(1)} %copy-done, s32[16,128]{1,0:T(8,128)S(1)} %bitcast.15), custom_call_target="tpu_custom_call" | custom-call | tf_op jit(solution)/shard_map/spread_weights/pallas_call | solution.py:363
  22.9 14.0 %all-to-all-done = f32[128,5,4,128]{3,2,1,0:T(4,128)S(1)} async-done(((f32[128,5,4,128]{3,2,1,0:T(4,128)}), f32[128,5,4,128]{3,2,1,0:T(4,128)S(1)}, u32[]{:S(2)}, u32[]{:S(2)}) %all-to-all-start) | async-done | bytes 1310752 | tf_op jit(solution)/shard_map/all_to_all | solution.py:328
  36.9 5.5 %couple.1 = f32[5120,128]{1,0:T(8,128)} custom-call(s32[2,512]{1,0:T(2,128)S(1)} %get-tuple-element.7.refs_0_, s32[2,1024]{1,0:T(2,128)S(1)} %get-tuple-element.8.refs_1_, bf16[1024,1024]{1,0:T(8,128)(2,1)S(1)} %get-tuple-element.9.refs_2_, f32[2560,128]{1,0:T(8,128)S(1)} %bitcast.13), custom_call_target="tpu_custom_call" | custom-call | tf_op jit(solution)/shard_map/couple/pallas_call | solution.py:377
  42.5 0.0 copy-start.5
  42.5 0.0 copy-start.3
  42.5 0.0 copy-start.4
  42.5 4.3 %all-to-all-start.1 = ((f32[128,10,4,128]{3,2,1,0:T(4,128)}), f32[128,10,4,128]{3,2,1,0:T(4,128)S(1)}, u32[]{:S(2)}, u32[]{:S(2)}) async-start(f32[128,10,4,128]{3,2,1,0:T(4,128)} %bitcast.9), calls=%async_computation.1 | async-start | bytes 5242880 | tf_op jit(solution)/shard_map/all_to_all | solution.py:328
  46.9 0.0 copy-done.5
  46.9 36.1 %all-to-all-done.1 = f32[128,10,4,128]{3,2,1,0:T(4,128)S(1)} async-done(((f32[128,10,4,128]{3,2,1,0:T(4,128)}), f32[128,10,4,128]{3,2,1,0:T(4,128)S(1)}, u32[]{:S(2)}, u32[]{:S(2)}) %all-to-all-start.1) | async-done | bytes 2621472 | tf_op jit(solution)/shard_map/all_to_all | solution.py:328
  83.0 0.0 copy-done.3
  83.0 0.0 copy-done.4
  83.0 2.8 %place.1 = (f32[320,1024]{1,0:T(8,128)}, f32[4,1024]{1,0:T(4,128)}) custom-call(s32[2,1024]{1,0:T(2,128)S(1)} %pad_add_fusion.refs_0_, s32[1,1024]{1,0:T(1,128)S(1)} %bitcast.14, f32[1,1024]{1,0:T(1,128)S(1)} %bitcast.16, f32[2,1024]{1,0:T(2,128)S(1)} %copy-done.3, f32[5120,128]{1,0:T(8,128)S(1)} %bitcast.12), custom_call_target="tpu_custom_call" | custom-call | tf_op jit(solution)/shard_map/place/pallas_call | solution.py:407
  (3 shorter events, 0.0 us)
Async XLA Ops:
  0.6 14.1 %copy-start.1 = (s32[4,512]{1,0:T(4,128)S(1)}, s32[4,512]{1,0:T(4,128)}, u32[]{:S(2)}) copy-start(s32[4,512]{1,0:T(4,128)} %refs_0_.1) | copy-start | bytes 24580
  0.6 14.1 %copy-start.2 = (s32[128,16]{0,1:T(8,128)S(1)}, s32[128,16]{0,1:T(8,128)}, u32[]{:S(2)}) copy-start(s32[128,16]{0,1:T(8,128)} %param.12) | copy-start | bytes 24580
  3.3 33.7 %all-to-all-start = ((f32[128,5,4,128]{3,2,1,0:T(4,128)}), f32[128,5,4,128]{3,2,1,0:T(4,128)S(1)}, u32[]{:S(2)}, u32[]{:S(2)}) async-start(f32[128,5,4,128]{3,2,1,0:T(4,128)} %bitcast.7), calls=%async_computation | async-start | bytes 2621440 | tf_op jit(solution)/shard_map/all_to_all | solution.py:328
  14.8 1.6 %copy-start = (f32[4,256,512]{2,1,0:T(8,128)S(1)}, f32[4,256,512]{2,1,0:T(8,128)}, u32[]{:S(2)}) copy-start(f32[4,256,512]{2,1,0:T(8,128)} %refs_1_.1) | copy-start | bytes 6291460
  42.5 4.4 %copy-start.5 = (s32[1024]{0:T(1024)S(1)}, s32[1024]{0:T(1024)}, u32[]{:S(2)}) copy-start(s32[1024]{0:T(1024)} %param.13) | copy-start | bytes 12292
  42.5 40.5 %copy-start.3 = (f32[2,1024]{1,0:T(2,128)S(1)}, f32[2,1024]{1,0:T(2,128)}, u32[]{:S(2)}) copy-start(f32[2,1024]{1,0:T(2,128)} %refs_3_.1) | copy-start | bytes 24580
  42.5 40.5 %copy-start.4 = (f32[1024]{0:T(1024)S(1)}, f32[1024]{0:T(1024)}, u32[]{:S(2)}) copy-start(f32[1024]{0:T(1024)} %param.14) | copy-start | bytes 12292
  42.5 40.5 %all-to-all-start.1 = ((f32[128,10,4,128]{3,2,1,0:T(4,128)}), f32[128,10,4,128]{3,2,1,0:T(4,128)S(1)}, u32[]{:S(2)}, u32[]{:S(2)}) async-start(f32[128,10,4,128]{3,2,1,0:T(4,128)} %bitcast.9), calls=%async_computation.1 | async-start | bytes 5242880 | tf_op jit(solution)/shard_map/all_to_all | solution.py:328
